TPU v7x, 512 devices: a whole 4x8x8 slice. The times are simulated.
512 devices in a mesh: seg: 16 (over x, y_hi), pen: 32 (over y_lo, z, core).
Axes of the slice: x: 4, y: 8 (y_hi: 4, y_lo: 2; y = y_hi * 2 + y_lo), z: 8, core: 2. Of those that a mesh axis runs over, the one named last changes fastest.
Arguments:
- state: float32 [64, 384, 384], P('seg', 'pen'), may hold values from -6 to 6
- krylov: float32 [16, 64, 384, 384], P(None, 'seg', 'pen'), may hold values from -15 to 15
Outputs:
- residual: float32 [64, 384, 384], P('seg', 'pen')
- next_vector: float32 [64, 384, 384], P('seg', 'pen')
- hessenberg: float32 [17], replicated
All inputs are finite; a program needn't handle non-finite values.
Results may differ from a plain program's by a relative error of at most 0.0003.
Values sent between devices are 32-bit elements; how exact they have to be, the bound alone decides.
No kernel may reach another device: no remote copies, remote signals or barrier semaphores. Data moves between devices by JAX's collectives and lax.ppermute only.
A program may use at most 64 MiB of HBM per device.

v0:
```python
import math

import jax
import jax.numpy as jnp
from jax import lax
from jax.sharding import PartitionSpec as P

NX = 384
NZ = 384
PLANES = 4
STEPS = 2
KRY = 16


time_step = 0.0003
viscosity = 0.0226


def shifted(block, axis, distance):
    devices = range(lax.axis_size(axis))
    route = [((i - distance) % len(devices), i) for i in devices]
    return lax.ppermute(block, axis, route)


def product(formula, former, latter):
    return jnp.einsum(
        formula, former, latter, precision=lax.Precision.HIGHEST, preferred_element_type=jnp.float32
    )


def tables(count):
    indices = jnp.arange(count, dtype=jnp.int32)
    phases = indices[:, None] * indices[None, :] % count
    angles = phases.astype(jnp.float32) * (2.0 * math.pi / count)
    cosines = jnp.cos(angles)
    sines = jnp.sin(angles)
    signed = jnp.where(indices <= count // 2, indices, indices - count).astype(jnp.float32)
    slopes = jnp.where(indices == count // 2, 0.0, signed)
    return (cosines + sines, slopes[:, None] * (cosines - sines), signed)


def tendency(z_slope, z_plain):
    stream_z = z_slope[0:2]
    vortex_z = z_slope[2:4]
    stream_x = z_plain[0:2]
    vortex_x = z_plain[2:4]
    base_term = stream_x[0] * vortex_z[0] - stream_z[0] * vortex_x[0]
    tangent_term = (
        stream_x[1] * vortex_z[0]
        + stream_x[0] * vortex_z[1]
        - stream_z[1] * vortex_x[0]
        - stream_z[0] * vortex_x[1]
    )
    return jnp.stack([base_term, tangent_term])


def advance(fields, inverse_k, damping, basis_x, slopes_x, basis_z, slopes_z, forward_x, forward_z):
    spectra = jnp.concatenate([fields * inverse_k, fields], 0)
    values_x = product("arzx,xj->arzj", spectra, basis_x)
    slopes_along = product("arzx,xj->arzj", spectra, slopes_x)
    z_slope = product(
        "arzx,zj->arxj",
        lax.all_to_all(values_x, "pen", split_axis=3, concat_axis=2, tiled=True),
        slopes_z,
    )
    z_plain = product(
        "arzx,zj->arxj",
        lax.all_to_all(slopes_along, "pen", split_axis=3, concat_axis=2, tiled=True),
        basis_z,
    )
    modes_z = product("arxz,zk->arxk", tendency(z_slope, z_plain), forward_z)
    returned = lax.all_to_all(modes_z, "pen", split_axis=3, concat_axis=2, tiled=True)
    forcing = product("arxz,xk->arzk", returned, forward_x)
    return (fields + time_step * forcing) * damping


def body(state, krylov):
    rank = lax.axis_index("pen")
    zcut = state.shape[1]
    basis_x, slopes_x, signed_x = tables(NX)
    basis_z, slopes_z, signed_z = tables(NZ)
    local_z = lax.dynamic_slice_in_dim(signed_z, rank * zcut, zcut)
    ksquare = local_z[:, None] ** 2 + signed_x[None, :] ** 2
    inverse_k = jnp.where(ksquare > 0, 1.0 / jnp.where(ksquare > 0, ksquare, 1.0), 0.0)
    damping = 1.0 / (1.0 + time_step * viscosity * ksquare)
    forward_x = basis_x / NX
    forward_z = basis_z / NZ
    direction = krylov[KRY - 1]
    fields = jnp.stack([state, direction])
    for repeat in range(STEPS):
        fields = advance(
            fields, inverse_k, damping, basis_x, slopes_x, basis_z, slopes_z, forward_x, forward_z
        )
    moved = shifted(fields, "seg", 1)
    residual = moved[0] - state
    image = moved[1] - direction
    total = float(lax.axis_size("seg") * PLANES * NZ * NX)
    local_dots = product("krzx,rzx->k", krylov, image)
    coeffs = lax.psum(local_dots, ("seg", "pen")) / total
    remain = image - product("k,krzx->rzx", coeffs, krylov)
    squared = lax.psum(jnp.sum(remain * remain), ("seg", "pen"))
    norm_value = jnp.sqrt(squared / total + 1e-06)
    return (residual, remain / norm_value, jnp.concatenate([coeffs, norm_value[None]]))


def solution(mesh):
    return jax.shard_map(
        body,
        mesh=mesh,
        in_specs=(P("seg", "pen", None), P(None, "seg", "pen", None)),
        out_specs=(P("seg", "pen", None), P("seg", "pen", None), P()),
        check_vma=False,
    )
```

profile of v0, /device:TPU:27, one launch (start us, length us, event | category | flops | bytes accessed | tf_op | source)
XLA Modules:
  0.0 439.5 jit_solution(11601115205310237027)
XLA Ops:
  0.7 0.9 slice.89
  1.6 0.9 copy.137
  2.6 0.7 fusion.81
  4.0 4.1 fusion.31
  8.1 3.1 copy.45
  11.1 5.0 %reshape.98 = f32[32,1,2304]{2,1,0:T(1,128)} reshape(f32[384,4,4,12]{3,2,1,0:T(4,128)S(1)} %bitcast.132) | data formatting | bytes 589824
  16.1 12.6 %all-to-all-start.1 = ((f32[32,1,2304]{2,1,0:T(1,128)}), f32[32,1,2304]{2,1,0:T(1,128)S(1)}, u32[]{:S(2)}, u32[]{:S(2)}) async-start(f32[32,1,2304]{2,1,0:T(1,128)} %reshape.98), calls=%async_computation.1 | async-start | bytes 589824 | tf_op jit(solution)/shard_map/all_to_all | solution.py:63
  28.8 5.2 %fusion.25 = f32[4,4,12,384]{3,2,1,0:T(8,128)} fusion(f32[384]{0:T(512)S(1)} %fusion.83, f32[1,4,12,384]{3,2,1,0:T(8,128)} %copy-done.3, f32[1,4,12,384]{3,2,1,0:T(8,128)} %bitcast.152, f32[2,4,12,384]{3,2,1,0:T(8,128)} %copy-done.8), kind=kOutput, calls=%fused_computation.32 | convolution fusion | flops 341508096 | bytes 591360 | tf_op jit(solution)/shard_map/arzx,xj->arzj/dot_general | solution.py:26
  33.9 3.1 copy.41
  37.0 5.0 %reshape.96 = f32[32,1,2304]{2,1,0:T(1,128)} reshape(f32[384,4,4,12]{3,2,1,0:T(4,128)S(1)} %bitcast.133) | data formatting | bytes 589824
  42.0 9.1 %all-to-all-start = ((f32[32,1,2304]{2,1,0:T(1,128)}), f32[32,1,2304]{2,1,0:T(1,128)}, u32[]{:S(2)}, u32[]{:S(2)}) async-start(f32[32,1,2304]{2,1,0:T(1,128)} %reshape.96), calls=%async_computation | async-start | bytes 589824 | tf_op jit(solution)/shard_map/all_to_all | solution.py:68
  51.6 2.1 reduce.1
  53.7 5.0 %reshape.99 = f32[384,4,4,12]{3,2,1,0:T(4,128)S(1)} reshape(f32[32,2304]{1,0:T(8,128)} %reduce.1) | data formatting | bytes 589824
  58.7 3.5 copy.133
  62.1 4.2 all_to_all.85
  66.4 4.1 fusion.23
  70.5 2.3 reduce
  72.8 4.2 reshape.97
  77.1 3.5 copy.134
  80.5 4.3 all_to_all.81
  84.8 3.3 fusion.33
  88.2 3.0 fusion.17
  91.2 0.8 copy.49
  92.1 2.0 reshape.100
  94.1 17.0 %all_to_all.108 = f32[32,1,1152]{2,1,0:T(1,128)S(1)} all-to-all(f32[32,1,1152]{2,1,0:T(1,128)S(1)} %reshape.100), channel_id=1, replica_groups=mesh['seg'=16,'pen'=32] {'pen'}, dimensions={0} | all-to-all | bytes 294912 | tf_op jit(solution)/shard_map/all_to_all | solution.py:72
  111.0 1.0 reduce.2
  112.0 2.1 reshape.101
  114.2 0.9 copy.136
  115.1 1.2 all_to_all.89
  116.4 3.0 broadcast_multiply_fusion
  120.1 4.1 fusion.27
  124.2 3.2 copy.57
  127.4 5.0 %reshape.104 = f32[32,1,2304]{2,1,0:T(1,128)} reshape(f32[384,4,4,12]{3,2,1,0:T(4,128)S(1)} %bitcast.138) | data formatting | bytes 589824
  132.4 4.7 %all-to-all-start.4 = ((f32[32,1,2304]{2,1,0:T(1,128)}), f32[32,1,2304]{2,1,0:T(1,128)S(1)}, u32[]{:S(2)}, u32[]{:S(2)}) async-start(f32[32,1,2304]{2,1,0:T(1,128)} %reshape.104), calls=%async_computation.4 | async-start | bytes 589824 | tf_op jit(solution)/shard_map/all_to_all | solution.py:63
  137.1 5.2 %fusion.21 = f32[4,4,12,384]{3,2,1,0:T(8,128)} fusion(f32[2,4,12,384]{3,2,1,0:T(8,128)} %copy-done.11, f32[2,4,12,384]{3,2,1,0:T(8,128)} %copy-done.13, f32[384]{0:T(512)S(1)} %fusion.83), kind=kOutput, calls=%fused_computation.28 | convolution fusion | flops 341434368 | bytes 591360 | tf_op jit(solution)/shard_map/arzx,xj->arzj/dot_general | solution.py:26
  142.3 3.1 copy.53
  145.3 5.0 %reshape.102 = f32[32,1,2304]{2,1,0:T(1,128)} reshape(f32[384,4,4,12]{3,2,1,0:T(4,128)S(1)} %bitcast.139) | data formatting | bytes 589824
  150.3 8.8 %all-to-all-start.3 = ((f32[32,1,2304]{2,1,0:T(1,128)}), f32[32,1,2304]{2,1,0:T(1,128)}, u32[]{:S(2)}, u32[]{:S(2)}) async-start(f32[32,1,2304]{2,1,0:T(1,128)} %reshape.102), calls=%async_computation.3 | async-start | bytes 589824 | tf_op jit(solution)/shard_map/all_to_all | solution.py:68
  159.1 2.1 reduce.4
  161.2 5.0 %reshape.105 = f32[384,4,4,12]{3,2,1,0:T(4,128)S(1)} reshape(f32[32,2304]{1,0:T(8,128)} %reduce.4) | data formatting | bytes 589824
  166.2 3.5 copy.131
  169.6 4.5 %all_to_all.97 = f32[4,4,384,12]{2,1,3,0:T(4,128)S(1)} reshape(f32[4,4,32,12,12]{3,2,1,4,0:T(8,128)} %bitcast.141) | data formatting | bytes 589824 | tf_op jit(solution)/shard_map/all_to_all | solution.py:63
  174.1 4.1 fusion.19
  178.3 2.3 reduce.3
  180.6 4.2 reshape.103
  184.8 3.5 copy.132
  188.3 4.2 all_to_all.93
  192.5 3.3 fusion.29
  195.9 3.0 fusion.14
  198.9 0.8 copy.61
  199.8 2.0 reshape.106
  201.8 16.8 %all_to_all.109 = f32[32,1,1152]{2,1,0:T(1,128)S(1)} all-to-all(f32[32,1,1152]{2,1,0:T(1,128)S(1)} %reshape.106), channel_id=1, replica_groups=mesh['seg'=16,'pen'=32] {'pen'}, dimensions={0} | all-to-all | bytes 294912 | tf_op jit(solution)/shard_map/all_to_all | solution.py:72
  218.6 1.0 reduce.5
  219.6 2.1 reshape.107
  221.7 0.9 copy.135
  222.6 1.2 all_to_all.101
  223.9 3.0 fusion.2
  226.9 4.7 %collective-permute-start = (f32[2,4,12,384]{3,2,1,0:T(8,128)S(1)}, f32[2,4,12,384]{3,2,1,0:T(8,128)S(1)}, u32[]{:S(2)}, u32[]{:S(2)}) collective-permute-start(f32[2,4,12,384]{3,2,1,0:T(8,128)S(1)} %fusion.2), channel_id=1, source_target_pairs={{480,0},{0,32},{32,64},{64,96},{96,128},{128,160},{160,192},{192,2... | collective-permute-start | bytes 442376 | tf_op jit(solution)/shard_map/ppermute | solution.py:22
  231.6 8.8 %collective-permute-done = f32[2,4,12,384]{3,2,1,0:T(8,128)S(1)} collective-permute-done((f32[2,4,12,384]{3,2,1,0:T(8,128)S(1)}, f32[2,4,12,384]{3,2,1,0:T(8,128)S(1)}, u32[]{:S(2)}, u32[]{:S(2)}) %collective-permute-start) | collective-permute-done | bytes 147488 | tf_op jit(solution)/shard_map/ppermute | solution.py:22
  240.4 1.7 fusion.8
  242.1 96.4 %psum.14 = f32[16]{0:T(128)S(1)} all-reduce(f32[16]{0:T(128)S(1)} %fusion.8), channel_id=1, replica_groups=mesh['seg'=16,'pen'=32] {'seg','pen'}, use_global_device_ids=true, to_apply=%region_0.1 | all-reduce | flops 16 | bytes 128 | tf_op jit(solution)/shard_map/psum | solution.py:99
  338.5 1.0 fusion.4
  340.1 96.5 %psum.15 = f32[]{:T(128)} all-reduce(f32[]{:T(128)} %multiply_reduce_fusion), channel_id=1, replica_groups=mesh['seg'=16,'pen'=32] {'seg','pen'}, use_global_device_ids=true, to_apply=%region_2.3 | all-reduce | flops 1 | bytes 8 | tf_op jit(solution)/shard_map/psum | solution.py:101
  437.3 0.7 copy.67
  (47 shorter events, 4.0 us)
Async XLA Ops:
  1.6 1.8 copy-start.3
  2.5 0.8 copy-start.5
  3.3 0.7 copy-start.8
  16.1 25.9 %all-to-all-start.1 = ((f32[32,1,2304]{2,1,0:T(1,128)}), f32[32,1,2304]{2,1,0:T(1,128)S(1)}, u32[]{:S(2)}, u32[]{:S(2)}) async-start(f32[32,1,2304]{2,1,0:T(1,128)} %reshape.98), calls=%async_computation.1 | async-start | bytes 589824 | tf_op jit(solution)/shard_map/all_to_all | solution.py:63
  42.0 28.5 %all-to-all-start = ((f32[32,1,2304]{2,1,0:T(1,128)}), f32[32,1,2304]{2,1,0:T(1,128)}, u32[]{:S(2)}, u32[]{:S(2)}) async-start(f32[32,1,2304]{2,1,0:T(1,128)} %reshape.96), calls=%async_computation | async-start | bytes 589824 | tf_op jit(solution)/shard_map/all_to_all | solution.py:68
  84.8 3.3 copy-start.2
  115.1 1.3 copy-start.4
  115.1 1.3 copy-start.6
  115.1 1.3 copy-start.9
  119.4 0.7 copy-start.13
  119.4 8.0 %copy-start.11 = (f32[2,4,12,384]{3,2,1,0:T(8,128)}, f32[2,4,12,384]{3,2,1,0:T(8,128)S(1)}, u32[]{:S(2)}) copy-start(f32[2,4,12,384]{3,2,1,0:T(8,128)S(1)} %get-tuple-element.21) | copy-start | bytes 442372
  132.4 17.9 %all-to-all-start.4 = ((f32[32,1,2304]{2,1,0:T(1,128)}), f32[32,1,2304]{2,1,0:T(1,128)S(1)}, u32[]{:S(2)}, u32[]{:S(2)}) async-start(f32[32,1,2304]{2,1,0:T(1,128)} %reshape.104), calls=%async_computation.4 | async-start | bytes 589824 | tf_op jit(solution)/shard_map/all_to_all | solution.py:63
  150.3 27.9 %all-to-all-start.3 = ((f32[32,1,2304]{2,1,0:T(1,128)}), f32[32,1,2304]{2,1,0:T(1,128)}, u32[]{:S(2)}, u32[]{:S(2)}) async-start(f32[32,1,2304]{2,1,0:T(1,128)} %reshape.102), calls=%async_computation.3 | async-start | bytes 589824 | tf_op jit(solution)/shard_map/all_to_all | solution.py:68
  192.5 3.3 copy-start.1
  222.6 1.3 copy-start.10
  222.6 1.3 copy-start.12
  223.9 16.5 %copy-start = (f32[16,4,12,384]{3,1,2,0:T(4,128)S(1)}, f32[16,4,12,384]{3,1,2,0:T(4,128)}, u32[]{:S(2)}) copy-start(f32[16,4,12,384]{3,1,2,0:T(4,128)} %param.3) | copy-start | bytes 3538948
  226.9 210.3 %copy-start.7 = (f32[4,12,384]{2,0,1:T(4,128)S(1)}, f32[4,12,384]{2,0,1:T(4,128)}, u32[]{:S(2)}) copy-start(f32[4,12,384]{2,0,1:T(4,128)} %param.2) | copy-start | bytes 221188
  226.9 13.5 %collective-permute-start = (f32[2,4,12,384]{3,2,1,0:T(8,128)S(1)}, f32[2,4,12,384]{3,2,1,0:T(8,128)S(1)}, u32[]{:S(2)}, u32[]{:S(2)}) collective-permute-start(f32[2,4,12,384]{3,2,1,0:T(8,128)S(1)} %fusion.2), channel_id=1, source_target_pairs={{480,0},{0,32},{32,64},{64,96},{96,128},{128,160},{160,192},{192,2... | collective-permute-start | bytes 442376 | tf_op jit(solution)/shard_map/ppermute | solution.py:22
where the time goes:
time: 447 us; the launch traced here: 439 us
  blocking collectives  227 us (51%)
  local copies, waits for them, and re-layouts  101 us (23%)
  matrix products  48 us (11%)
  starting transfers between devices  39.8 us (9%)
  other arithmetic  12.9 us (3%)
  waiting for transfers between devices  8.79 us (2%)
    psum x1, blocking collectives, body(): squared = lax.psum(jnp.sum(remain * remain), ('seg', 'pen'))  96.5 us
    psum x1, blocking collectives, body(): coeffs = lax.psum(local_dots, ('seg', 'pen')) / total  96.4 us
    unnamed x44, local copies, waits for them, and re-layouts  50.3 us
    dot_general x14, matrix products, product(): jnp.einsum(formula, former, latter, precision=lax.Precision.HIGHEST, pref...  48 us
    all_to_all x2, blocking collectives, advance(): lax.all_to_all(modes_z, 'pen', split_axis=3, concat_axis=2, tiled=True)  33.7 us
    all_to_all x2, starting transfers between devices, advance(): lax.all_to_all(slopes_along, 'pen', split_axis=3, concat_axis=2, tiled=True)  17.8 us
    all_to_all x2, starting transfers between devices, advance(): lax.all_to_all(values_x, 'pen', split_axis=3, concat_axis=2, tiled=True)  17.3 us
    all_to_all x5, local copies, waits for them, and re-layouts, advance(): lax.all_to_all(slopes_along, 'pen', split_axis=3, concat_axis=2, tiled=True)  16 us
  transfers between devices with their start and end apart: 5, of which 1 were waited for; matrix products, arithmetic and copies ran while one was open for 13% of the time, Pallas kernels for 0%

commit v1 on v0

v1 whole, which is shorter than its diff:
```python
import functools

import jax
import jax.numpy as jnp
import numpy as np
from jax import lax
from jax.experimental import pallas as pl
from jax.experimental.pallas import tpu as pltpu
from jax.sharding import PartitionSpec as P

NX = 384
NZ = 384
PLANES = 4
STEPS = 2
KRY = 16
SEGS = 16
PEN = 32
CUT = NZ // PEN
TEAM = 8
WIDE = NZ // TEAM
TILE = 128
INTERPRET = False

time_step = 0.0003
viscosity = 0.0226


def pen_index(y, team, member):
    return 16 * y + 4 * team + member


TEAMS = [[pen_index(y, q, r) for y in range(2) for r in range(4)] for q in range(4)]
PEERS = [[pen_index(y, q, r) for q in range(4)] for y in range(2) for r in range(4)]


def row_order():
    rows = []
    for y in range(2):
        for r in range(4):
            for q in range(4):
                rows += [CUT * pen_index(y, q, r) + n for n in range(CUT)]
    return np.array(rows)


def split_table(table):
    high = np.asarray(table, dtype=np.float32).astype(jnp.bfloat16)
    low = np.asarray(table - high.astype(np.float64), dtype=np.float32).astype(jnp.bfloat16)
    return np.concatenate([high, low], 0)


@functools.lru_cache(None)
def tables():
    count = NX
    k = np.arange(count)
    angle = 2.0 * np.pi * (np.outer(k, k) % count) / count
    cas = np.cos(angle) + np.sin(angle)
    signed = np.where(k <= count // 2, k, k - count)
    slopes = np.where(k == count // 2, 0, signed)
    slope = slopes[:, None] * (np.cos(angle) - np.sin(angle))
    order = row_order()
    pick = np.ix_(order, order)
    return (
        split_table(cas),
        split_table(slope),
        split_table(cas[pick]),
        split_table(slope[pick].T),
    )


def halves(value):
    high = value.astype(jnp.bfloat16)
    low = (value - high.astype(jnp.float32)).astype(jnp.bfloat16)
    return high, low


def mm(a, b):
    return jnp.dot(a, b, preferred_element_type=jnp.float32)


def times_table(value, table_ref):
    high, low = halves(value)
    n = value.shape[0]
    upper = table_ref[0:NX, :]
    both = mm(jnp.concatenate([high, low], 0), upper)
    return both[0:n] + both[n : 2 * n] + mm(high, table_ref[NX : 2 * NX, :])


def table_times(table_ref, value):
    high, low = halves(value)
    both = mm(table_ref[...], high)
    return both[0:NX] + both[NX : 2 * NX] + mm(table_ref[0:NX, :], low)


def call(kernel, outs, scratch=(), flops=0, moved=0):
    return pl.pallas_call(
        kernel,
        out_shape=outs,
        scratch_shapes=list(scratch),
        cost_estimate=pl.CostEstimate(flops=flops, bytes_accessed=moved, transcendentals=0),
        interpret=INTERPRET,
    )


def f32(*shape):
    return jax.ShapeDtypeStruct(shape, jnp.float32)


def tile(t):
    return slice(TILE * t, TILE * (t + 1))


def gather_rows(state_ref, last_ref, out_ref):
    for q in range(4):
        for member, ref in enumerate((state_ref, last_ref)):
            for t in range(3):
                row = 36 * member + CUT * t
                out_ref[q, row : row + CUT, :] = ref[:, q, tile(t)]


def spread(fields, inverse_ref, cas_ref, slope_ref, send_ref):
    base, tangent = fields
    inverse = inverse_ref[...]
    spectra = jnp.concatenate([base * inverse, tangent * inverse, base, tangent], 0)
    values = times_table(spectra, cas_ref)
    slopes = times_table(spectra, slope_ref)
    for m in range(TEAM):
        cut = slice(WIDE * m, WIDE * (m + 1))
        parts = [values[WIDE * k : WIDE * (k + 1), cut] for k in range(4)]
        parts += [slopes[WIDE * k : WIDE * (k + 1), cut] for k in range(4)]
        block = jnp.concatenate(parts, 1)
        for t in range(3):
            send_ref[m, WIDE * t : WIDE * (t + 1), :] = block[:, tile(t)]


def first_kernel(recv_ref, inverse_ref, cas_ref, slope_ref, send_ref, fields_ref):
    for q in range(4):
        for member in range(2):
            for t in range(3):
                row = 36 * member + CUT * t
                fields_ref[member, CUT * q : CUT * (q + 1), tile(t)] = recv_ref[
                    q, row : row + CUT, :
                ]
    spread((fields_ref[0], fields_ref[1]), inverse_ref, cas_ref, slope_ref, send_ref)


def grid_kernel(recv_ref, cas_ref, slope_ref, send_ref):
    tiles = [
        jnp.concatenate([recv_ref[m, WIDE * t : WIDE * (t + 1), :] for m in range(TEAM)], 0)
        for t in range(3)
    ]
    along_z = table_times(slope_ref, jnp.concatenate(tiles[0:2], 1))
    along_x = table_times(cas_ref, jnp.concatenate(tiles[1:3], 1))
    pair = 2 * WIDE
    psi_z = along_z[:, 0:pair]
    vort_z = along_z[:, pair : 2 * pair]
    psi_x = along_x[:, 64 : 64 + pair]
    vort_x = along_x[:, 64 + pair : 64 + 2 * pair]

    def twice(x):
        return jnp.concatenate([x[:, 0:WIDE], x[:, 0:WIDE]], 1)

    first = psi_x * twice(vort_z) - psi_z * twice(vort_x)
    second = psi_x[:, 0:WIDE] * vort_z[:, WIDE:pair] - psi_z[:, 0:WIDE] * vort_x[:, WIDE:pair]
    zero = jnp.zeros((NZ, WIDE), jnp.float32)
    total = jnp.concatenate([first, jnp.zeros((NZ, TILE - pair), jnp.float32)], 1)
    total = total + jnp.concatenate([zero, second, jnp.zeros((NZ, TILE - pair), jnp.float32)], 1)
    modes = table_times(cas_ref, total)
    for m in range(TEAM):
        send_ref[m] = modes[WIDE * m : WIDE * (m + 1), :]


def advanced(recv_ref, fields_ref, damping_ref, cas_ref):
    lines = [
        jnp.concatenate(
            [recv_ref[m, :, WIDE * member : WIDE * (member + 1)] for m in range(TEAM)], 1
        )
        for member in range(2)
    ]
    forcing = times_table(jnp.concatenate(lines, 0), cas_ref)
    scale = time_step / (NX * NZ)
    damping = damping_ref[...]
    return [
        (fields_ref[member] + scale * forcing[WIDE * member : WIDE * (member + 1)]) * damping
        for member in range(2)
    ]


def middle_kernel(
    recv_ref, old_ref, damping_ref, inverse_ref, cas_ref, slope_ref, send_ref, fields_ref
):
    fields = advanced(recv_ref, old_ref, damping_ref, cas_ref)
    fields_ref[0] = fields[0]
    fields_ref[1] = fields[1]
    spread(fields, inverse_ref, cas_ref, slope_ref, send_ref)


def last_kernel(team_ref, recv_ref, old_ref, damping_ref, cas_ref, *refs):
    outs, keep = refs[:8], refs[8]
    fields = advanced(recv_ref, old_ref, damping_ref, cas_ref)
    for member in range(2):
        for q in range(4):
            for t in range(3):
                keep[member, q, CUT * t : CUT * (t + 1), :] = fields[member][
                    CUT * q : CUT * (q + 1), tile(t)
                ]
    for member in range(2):
        for d in range(4):
            outs[4 * member + d][...] = keep[member, lax.rem(team_ref[0] + d, 4)]


def row_sums(value):
    ones = jnp.ones((8, TILE), jnp.bfloat16)
    first = value.astype(jnp.bfloat16)
    rest = value - first.astype(jnp.float32)
    second = rest.astype(jnp.bfloat16)
    third = (rest - second.astype(jnp.float32)).astype(jnp.bfloat16)
    dims = (((1,), (1,)), ((), ()))
    total = jnp.zeros((8, value.shape[0]), jnp.float32)
    for part in (third, second, first):
        total = total + lax.dot_general(ones, part, dims, preferred_element_type=jnp.float32)
    return total


def fold(value):
    return jnp.sum(value, axis=0, keepdims=True)


def fold(value):
    line = value[:, tile(0)] + value[:, tile(1)] + value[:, tile(2)]
    return jnp.sum(line, axis=0, keepdims=True)


def gram_kernel(kry_ref, out_ref, keep):
    for a in range(0, KRY, 4):
        for b in range(0, a + 1, 4):

            def step(g, sums):
                left = [kry_ref[a + i, g] for i in range(4)]
                right = [kry_ref[b + j, g] for j in range(4)]
                pairs = [(i, j) for i in range(4) for j in range(4)]
                return tuple(sums[4 * i + j] + left[i] * right[j] for i, j in pairs)

            zero = jnp.zeros((PLANES, NX), jnp.float32)
            sums = lax.fori_loop(0, CUT, step, (zero,) * 16)
            for i in range(4):
                for j in range(4):
                    line = fold(sums[4 * i + j])
                    keep[KRY * (a + i) + b + j : KRY * (a + i) + b + j + 1, :] = line
                    if a != b:
                        keep[KRY * (b + j) + a + i : KRY * (b + j) + a + i + 1, :] = line
    packed = row_sums(keep[...])
    row = lax.broadcasted_iota(jnp.int32, (8, TILE), 0)
    out_ref[...] = jnp.where(
        row == 1, packed[:, 0:TILE], jnp.where(row == 2, packed[:, TILE : 2 * TILE], 0.0)
    )


def place(team_ref, parts, out_ref, order):
    for d in range(4):
        order[lax.rem(team_ref[0] + 4 - d, 4)] = parts[d][...]
    for p in range(PLANES):
        for t in range(3):
            out_ref[:, p, tile(t)] = order[p, CUT * t : CUT * (t + 1), :]


def dots_kernel(team_ref, kry_ref, gram_ref, *refs):
    parts, image_ref, out_ref, keep, order = refs[:4], refs[4], refs[5], refs[6], refs[7]
    place(team_ref, parts, image_ref, order)
    image = image_ref[...] - kry_ref[KRY - 1]
    image_ref[...] = image
    keep[...] = jnp.zeros_like(keep)
    for k in range(KRY):
        keep[k : k + 1, :] = fold(jnp.sum(kry_ref[k] * image, axis=0))
    keep[KRY : KRY + 1, :] = fold(jnp.sum(image * image, axis=0))
    packed = row_sums(keep[...])
    row = lax.broadcasted_iota(jnp.int32, (8, TILE), 0)
    out_ref[...] = jnp.where(row == 0, packed, gram_ref[...])


def finish_kernel(team_ref, sums_ref, kry_ref, image_ref, state_ref, *refs):
    parts, residual_ref, next_ref, hess_ref, order = refs[:4], refs[4], refs[5], refs[6], refs[7]
    place(team_ref, parts, residual_ref, order)
    residual_ref[...] = residual_ref[...] - state_ref[...]
    total = float(SEGS * PLANES * NZ * NX)
    sums = sums_ref[0]
    for s in range(1, sums_ref.shape[0]):
        sums = sums + sums_ref[s]
    sums = sums / total
    coeffs = [sums[0:1, k : k + 1] for k in range(KRY)]
    remain = image_ref[...]
    for k in range(KRY):
        remain = remain - coeffs[k] * kry_ref[k]
    lane = lax.broadcasted_iota(jnp.int32, (1, TILE), 1)
    inner = jnp.zeros((1, TILE), jnp.float32)
    outer = [inner, inner]
    for k in range(KRY):
        inner = jnp.where(lane % KRY == k, coeffs[k], inner)
        half, block = k // 8, k % 8
        outer[half] = jnp.where(lane // KRY == block, coeffs[k], outer[half])
    line = jnp.where(lane < KRY, sums[0:1] * sums[0:1], 0.0)
    quadratic = inner * (outer[0] * sums[1:2] + outer[1] * sums[2:3]) - 2.0 * line
    squared = sums[0:1, KRY : KRY + 1] + jnp.sum(quadratic, axis=1, keepdims=True)
    norm = jnp.sqrt(jnp.maximum(squared, 0.0) + 1e-06)
    next_ref[...] = remain / norm
    hess = jnp.where(lane == KRY, norm, sums[0:1])
    hess_ref[...] = jnp.broadcast_to(hess, (8, TILE))


def route(distance, segs):
    pairs = []
    for s in range(segs):
        for y in range(2):
            for q in range(4):
                for r in range(4):
                    here = s * PEN + pen_index(y, q, r)
                    there = (s + 1) % segs * PEN + pen_index(y, (q + distance) % 4, r)
                    pairs.append((here, there))
    return pairs


def gathered(value, axis):
    size = lax.axis_size(axis)
    copies = jnp.broadcast_to(value[None], (size,) + value.shape)
    return lax.all_to_all(copies, axis, 0, 0, tiled=True)


def body(state, krylov):
    pen = lax.axis_index("pen")
    segs = lax.axis_size("seg")
    team = (pen // 4) % 4
    numbers = np.arange(NX)
    signed = np.where(numbers <= NX // 2, numbers, numbers - NX).astype(np.float32)
    steps = np.arange(WIDE)
    rows = CUT * (16 * (pen // 16) + pen % 4) + (4 * CUT * (steps // CUT) + steps % CUT)
    mode = jnp.where(rows <= NZ // 2, rows, rows - NZ).astype(jnp.float32)
    ksquare = mode[:, None] ** 2 + signed[None, :] ** 2
    inverse = jnp.where(ksquare > 0, 1.0 / jnp.where(ksquare > 0, ksquare, 1.0), 0.0)
    damping = 1.0 / (1.0 + time_step * viscosity * ksquare)
    cas, slope, cas_z, slope_z = [jnp.asarray(t) for t in tables()]
    team_ref = team.astype(jnp.int32).reshape(1)
    smem = pl.BlockSpec(memory_space=pltpu.SMEM)
    vmem = pl.BlockSpec(memory_space=pltpu.VMEM)

    state_f = state.transpose(1, 0, 2)
    kry_f = krylov.transpose(0, 2, 1, 3)
    exchange = functools.partial(
        lax.all_to_all, axis_name="pen", split_axis=0, concat_axis=0, tiled=True
    )

    whole = pl.BlockSpec((CUT, PLANES, NX), lambda i: (0, 0, 0))
    last = pl.BlockSpec((None, CUT, PLANES, NX), lambda i: (KRY - 1, 0, 0, 0))
    packed = pl.pallas_call(
        gather_rows,
        grid=(1,),
        in_specs=[whole, last],
        out_specs=pl.BlockSpec((4, 72, TILE), lambda i: (0, 0, 0)),
        out_shape=f32(4, 72, TILE),
        interpret=INTERPRET,
    )(state_f, kry_f)
    packed = exchange(packed, axis_index_groups=PEERS)
    gram = call(
        gram_kernel,
        f32(8, TILE),
        [pltpu.VMEM((KRY * KRY, TILE), jnp.float32)],
        flops=10_000_000,
        moved=1_300_000,
    )(kry_f)
    send, fields = call(
        first_kernel, (f32(TEAM, 144, TILE), f32(2, WIDE, NX)), flops=700_000_000, moved=3_000_000
    )(packed, inverse, cas, slope)
    for repeat in range(STEPS):
        recv = exchange(send, axis_index_groups=TEAMS)
        modes = call(
            grid_kernel, f32(TEAM, WIDE, TILE), flops=900_000_000, moved=2_500_000
        )(recv, cas_z, slope_z)
        recv = exchange(modes, axis_index_groups=TEAMS)
        if repeat < STEPS - 1:
            send, fields = call(
                middle_kernel,
                (f32(TEAM, 144, TILE), f32(2, WIDE, NX)),
                flops=900_000_000,
                moved=3_000_000,
            )(recv, fields, damping, inverse, cas, slope)
    pieces = pl.pallas_call(
        last_kernel,
        in_specs=[smem] + [vmem] * 4,
        out_specs=[vmem] * 8,
        out_shape=[f32(36, TILE)] * 8,
        scratch_shapes=[pltpu.VMEM((2, 4, 36, TILE), jnp.float32)],
        cost_estimate=pl.CostEstimate(flops=200_000_000, bytes_accessed=1_500_000, transcendentals=0),
        interpret=INTERPRET,
    )(team_ref, recv, fields, damping, cas)
    tangent = [lax.ppermute(pieces[4 + d], ("seg", "pen"), route(d, segs)) for d in range(4)]
    base = [lax.ppermute(pieces[d], ("seg", "pen"), route(d, segs)) for d in range(4)]
    image, partial = pl.pallas_call(
        dots_kernel,
        in_specs=[smem] + [vmem] * 6,
        out_specs=[vmem] * 2,
        out_shape=[f32(CUT, PLANES, NX), f32(8, TILE)],
        scratch_shapes=[
            pltpu.VMEM((TILE, TILE), jnp.float32),
            pltpu.VMEM((4, 36, TILE), jnp.float32),
        ],
        cost_estimate=pl.CostEstimate(flops=1_000_000, bytes_accessed=1_300_000, transcendentals=0),
        interpret=INTERPRET,
    )(team_ref, kry_f, gram, *tangent)
    sums = gathered(partial, "pen")
    sums = gathered(jnp.sum(sums, axis=0), "seg")
    residual, vector, hess = pl.pallas_call(
        finish_kernel,
        in_specs=[smem] + [vmem] * 8,
        out_specs=[vmem] * 3,
        out_shape=[f32(CUT, PLANES, NX)] * 2 + [f32(8, TILE)],
        scratch_shapes=[pltpu.VMEM((4, 36, TILE), jnp.float32)],
        cost_estimate=pl.CostEstimate(flops=1_000_000, bytes_accessed=1_500_000, transcendentals=0),
        interpret=INTERPRET,
    )(team_ref, sums, kry_f, image, state_f, *base)
    return (residual.transpose(1, 0, 2), vector.transpose(1, 0, 2), hess[0, : KRY + 1])


def solution(mesh):
    return jax.shard_map(
        body,
        mesh=mesh,
        in_specs=(P("seg", "pen", None), P(None, "seg", "pen", None)),
        out_specs=(P("seg", "pen", None), P("seg", "pen", None), P()),
        check_vma=False,
    )
```

time: 447 us -> 174 us (0.39)
  the two profiles are of different devices: /device:TPU:27 before, /device:TPU:8 now
where the time goes in v1:
time: 174 us; the launch traced here: 173 us
  starting transfers between devices  60.1 us (35%)
  blocking collectives  53.6 us (31%)
  Pallas kernels  27.4 us (16%)
  waiting for transfers between devices  25.2 us (14%)
  local copies, waits for them, and re-layouts  5.09 us (3%)
    all_to_all x2, blocking collectives, body(): recv = exchange(send, axis_index_groups=TEAMS)  27.6 us
    ppermute x4, starting transfers between devices, body(): lax.ppermute(pieces[d], ('seg', 'pen'), route(d, segs))  19.4 us
    ppermute x4, starting transfers between devices, body(): lax.ppermute(pieces[4 + d], ('seg', 'pen'), route(d, segs))  19 us
    all_to_all x1, blocking collectives, gathered(): return lax.all_to_all(copies, axis, 0, 0, tiled=True)  15.8 us
    all_to_all x1, starting transfers between devices, body(): packed = exchange(packed, axis_index_groups=PEERS)  10.3 us
    all_to_all x1, blocking collectives, body(): recv = exchange(modes, axis_index_groups=TEAMS)  10.1 us
    all_to_all x1, waiting for transfers between devices, body(): packed = exchange(packed, axis_index_groups=PEERS)  8.81 us
    ppermute x4, waiting for transfers between devices, body(): lax.ppermute(pieces[d], ('seg', 'pen'), route(d, segs))  7.71 us
  transfers between devices with their start and end apart: 11, of which 6 were waited for; matrix products, arithmetic and copies ran while one was open for 0% of the time, Pallas kernels for 2%

profile of v1, /device:TPU:8, one launch (start us, length us, event | category | flops | bytes accessed | tf_op | source)
XLA Modules:
  0.0 173.0 jit_solution(2785667584556133078)
XLA Ops:
  0.6 0.0 copy-start.16
  0.6 0.0 copy-start.11
  0.7 1.7 shard_map.104
  2.3 10.3 %all-to-all-start = ((f32[4,72,128]{2,1,0:T(8,128)}), f32[4,72,128]{2,1,0:T(8,128)S(1)}, u32[]{:S(2)}, u32[]{:S(2)}) async-start(f32[4,72,128]{2,1,0:T(8,128)} %shard_map.104), calls=%async_computation | async-start | bytes 294912 | tf_op jit(solution)/shard_map/all_to_all | solution.py:360
  12.6 0.0 copy-done.16
  12.6 0.0 copy-done.11
  12.6 0.8 fusion.3
  13.4 8.8 %all-to-all-done.recv_ref = f32[4,72,128]{2,1,0:T(8,128)S(1)} async-done(((f32[4,72,128]{2,1,0:T(8,128)}), f32[4,72,128]{2,1,0:T(8,128)S(1)}, u32[]{:S(2)}, u32[]{:S(2)}) %all-to-all-start) | async-done | bytes 147488 | tf_op jit(solution)/shard_map/all_to_all | solution.py:360
  22.2 0.0 copy-start.2
  22.2 0.7 copy-done.2
  22.9 3.1 %shard_map.105 = (f32[8,144,128]{2,1,0:T(8,128)}, f32[2,48,384]{2,1,0:T(8,128)}) custom-call(f32[4,72,128]{2,1,0:T(8,128)} %copy-done.2, f32[48,384]{1,0:T(8,128)} %get-tuple-element.38.inverse_ref, bf16[768,384]{1,0:T(8,128)(2,1)} %constant.74.clone.cas_ref, bf16[768,384]{1,0:T(8,128)(2,1)} %constant.75.clone.slope_ref), custom_call_target="tpu_custom_call" | custom-call | flops 700000000 | bytes 3000000 | tf_op jit(solution)/shard_map/pallas_call | solution.py:368
  26.0 13.6 %all_to_all.35.recv_ref = f32[8,144,128]{2,1,0:T(8,128)} all-to-all(f32[8,144,128]{2,1,0:T(8,128)} %get-tuple-element.20), channel_id=1, replica_groups={{0,1,2,3,16,17,18,19},{4,5,6,7,20,21,22,23},{8,9,10,11,24,25,26,27},{12..., dimensions={0} | all-to-all | bytes 1179648 | tf_op jit(solution)/shard_map/all_to_all | solution.py:372
  39.6 3.8 %shard_map.106 = f32[8,48,128]{2,1,0:T(8,128)} custom-call(f32[8,144,128]{2,1,0:T(8,128)} %all_to_all.35.recv_ref, bf16[768,384]{1,0:T(8,128)(2,1)} %constant.76.clone.cas_ref, bf16[768,384]{1,0:T(8,128)(2,1)} %constant.77.clone.slope_ref), custom_call_target="tpu_custom_call" | custom-call | flops 900000000 | bytes 2500000 | tf_op jit(solution)/shard_map/pallas_call | solution.py:373
  43.4 10.1 %all_to_all.36.recv_ref = f32[8,48,128]{2,1,0:T(8,128)} all-to-all(f32[8,48,128]{2,1,0:T(8,128)} %shard_map.106), channel_id=1, replica_groups={{0,1,2,3,16,17,18,19},{4,5,6,7,20,21,22,23},{8,9,10,11,24,25,26,27},{12..., dimensions={0} | all-to-all | bytes 393216 | tf_op jit(solution)/shard_map/all_to_all | solution.py:376
  53.5 3.6 %shard_map.107 = (f32[8,144,128]{2,1,0:T(8,128)}, f32[2,48,384]{2,1,0:T(8,128)}) custom-call(f32[8,48,128]{2,1,0:T(8,128)} %all_to_all.36.recv_ref, f32[2,48,384]{2,1,0:T(8,128)} %get-tuple-element.21.old_ref, f32[48,384]{1,0:T(8,128)} %get-tuple-element.37.damping_ref, f32[48,384]{1,0:T(8,128)} %get-tuple-element.38.inverse_ref, ...), custom_call_target="tpu_custom_call" | custom-call | flops 900000000 | bytes 3000000 | tf_op jit(solution)/shard_map/pallas_call | solution.py:378
  57.1 14.1 %all_to_all.37.recv_ref = f32[8,144,128]{2,1,0:T(8,128)} all-to-all(f32[8,144,128]{2,1,0:T(8,128)} %get-tuple-element.22), channel_id=1, replica_groups={{0,1,2,3,16,17,18,19},{4,5,6,7,20,21,22,23},{8,9,10,11,24,25,26,27},{12..., dimensions={0} | all-to-all | bytes 1179648 | tf_op jit(solution)/shard_map/all_to_all | solution.py:372
  71.2 3.8 %shard_map.108 = f32[8,48,128]{2,1,0:T(8,128)} custom-call(f32[8,144,128]{2,1,0:T(8,128)} %all_to_all.37.recv_ref, bf16[768,384]{1,0:T(8,128)(2,1)} %constant.76.clone.cas_ref, bf16[768,384]{1,0:T(8,128)(2,1)} %constant.77.clone.slope_ref), custom_call_target="tpu_custom_call" | custom-call | flops 900000000 | bytes 2500000 | tf_op jit(solution)/shard_map/pallas_call | solution.py:373
  75.0 4.7 %all-to-all-start.4 = ((f32[8,48,128]{2,1,0:T(8,128)}), f32[8,48,128]{2,1,0:T(8,128)S(1)}, u32[]{:S(2)}, u32[]{:S(2)}) async-start(f32[8,48,128]{2,1,0:T(8,128)} %shard_map.108), calls=%async_computation.4 | async-start | bytes 393216 | tf_op jit(solution)/shard_map/all_to_all | solution.py:376
  79.7 4.8 %all-to-all-done.4.recv_ref = f32[8,48,128]{2,1,0:T(8,128)S(1)} async-done(((f32[8,48,128]{2,1,0:T(8,128)}), f32[8,48,128]{2,1,0:T(8,128)S(1)}, u32[]{:S(2)}, u32[]{:S(2)}) %all-to-all-start.4) | async-done | bytes 196640 | tf_op jit(solution)/shard_map/all_to_all | solution.py:376
  84.5 0.7 copy-done
  85.2 2.3 %shard_map.109 = (f32[36,128]{1,0:T(8,128)}, f32[36,128]{1,0:T(8,128)}, f32[36,128]{1,0:T(8,128)}, f32[36,128]{1,0:T(8,128)}, f32[36,128]{1,0:T(8,128)}, /*index...) custom-call(s32[1]{0:T(128)} %bitcast.team_ref, f32[8,48,128]{2,1,0:T(8,128)} %copy-done, ...), custom_call_target="tpu_custom_call" | custom-call | flops 200000000 | bytes 1500000 | tf_op jit(solution)/shard_map/pallas_call | solution.py:384
  87.5 4.5 %collective-permute-start = (f32[36,128]{1,0:T(8,128)}, f32[36,128]{1,0:T(8,128)S(1)}, u32[]{:S(2)}, u32[]{:S(2)}) collective-permute-start(f32[36,128]{1,0:T(8,128)} %get-tuple-element.24), channel_id=1, source_target_pairs={{0,32},{1,33},{2,34},{3,35},{4,36},{5,37},{6,38},{7,39},{8,40},{9,... | collective-permute-start | bytes 55304 | tf_op jit(solution)/shard_map/ppermute | solution.py:393
  92.0 5.3 %collective-permute-start.1 = (f32[36,128]{1,0:T(8,128)}, f32[36,128]{1,0:T(8,128)S(1)}, u32[]{:S(2)}, u32[]{:S(2)}) collective-permute-start(f32[36,128]{1,0:T(8,128)} %get-tuple-element.25), channel_id=1, source_target_pairs={{0,36},{1,37},{2,38},{3,39},{4,40},{5,41},{6,42},{7,43},{8,44},{9,... | collective-permute-start | bytes 55304 | tf_op jit(solution)/shard_map/ppermute | solution.py:393
  97.3 4.7 %collective-permute-start.2 = (f32[36,128]{1,0:T(8,128)}, f32[36,128]{1,0:T(8,128)S(1)}, u32[]{:S(2)}, u32[]{:S(2)}) collective-permute-start(f32[36,128]{1,0:T(8,128)} %get-tuple-element.26), channel_id=1, source_target_pairs={{0,40},{1,41},{2,42},{3,43},{4,44},{5,45},{6,46},{7,47},{8,32},{9,... | collective-permute-start | bytes 55304 | tf_op jit(solution)/shard_map/ppermute | solution.py:393
  102.0 4.5 %collective-permute-start.3 = (f32[36,128]{1,0:T(8,128)}, f32[36,128]{1,0:T(8,128)S(1)}, u32[]{:S(2)}, u32[]{:S(2)}) collective-permute-start(f32[36,128]{1,0:T(8,128)} %get-tuple-element.27), channel_id=1, source_target_pairs={{0,44},{1,45},{2,46},{3,47},{4,32},{5,33},{6,34},{7,35},{8,36},{9,... | collective-permute-start | bytes 55304 | tf_op jit(solution)/shard_map/ppermute | solution.py:393
  106.5 4.2 %shard_map.103.gram_ref = f32[8,128]{1,0:T(8,128)} custom-call(f32[16,12,4,384]{3,2,1,0:T(4,128)} %bitcast.8), custom_call_target="tpu_custom_call" | custom-call | flops 10000000 | bytes 1300000 | tf_op jit(solution)/shard_map/pallas_call | solution.py:361
  110.8 0.0 collective-permute-done.refs_0_
  110.8 0.0 copy-start.6
  110.8 0.0 collective-permute-done.1.refs_1_
  110.8 0.0 copy-start.8
  110.8 1.4 collective-permute-done.2.refs_2_
  112.2 2.5 %collective-permute-done.3.refs_3_ = f32[36,128]{1,0:T(8,128)S(1)} collective-permute-done((f32[36,128]{1,0:T(8,128)}, f32[36,128]{1,0:T(8,128)S(1)}, u32[]{:S(2)}, u32[]{:S(2)}) %collective-permute-start.3) | collective-permute-done | bytes 18464 | tf_op jit(solution)/shard_map/ppermute | solution.py:393
  114.7 0.0 copy-done.6
  114.7 0.0 copy-done.8
  114.7 0.0 copy-done.9
  114.7 0.0 copy-start.10
  114.8 0.6 copy-done.10
  115.3 2.4 %shard_map.110 = (f32[12,4,384]{2,1,0:T(4,128)}, f32[8,128]{1,0:T(8,128)}) custom-call(s32[1]{0:T(128)} %bitcast.team_ref, f32[16,12,4,384]{3,2,1,0:T(4,128)} %bitcast.9, f32[8,128]{1,0:T(8,128)} %shard_map.103.gram_ref, f32[36,128]{1,0:T(8,128)} %copy-done.6, f32[36,128]{1,0:T(8,128)} %copy-done.8, f32[36,128]{1,0:T(8,128)} %copy-done.9, f32[36,128]{1,0:T(8,128)} %copy-done.10), custom_call_target="tpu_custom_call" | custom-call | flops 1000000 | bytes 1300000 | tf_op jit(solution)/shard_map/pallas_call | solution.py:395
  117.8 0.7 broadcast_in_dim.7
  118.5 15.8 %all_to_all.38 = f32[32,8,128]{2,1,0:T(8,128)S(1)} all-to-all(f32[32,8,128]{2,1,0:T(8,128)S(1)} %broadcast_in_dim.7), channel_id=1, replica_groups=mesh['seg'=16,'pen'=32] {'pen'}, dimensions={0} | all-to-all | bytes 262144 | tf_op jit(solution)/shard_map/all_to_all | solution.py:324
  134.3 0.6 broadcast_in_dim.8
  135.0 6.7 %all-to-all-start.6 = ((f32[16,8,128]{2,1,0:T(8,128)}), f32[16,8,128]{2,1,0:T(8,128)S(1)}, u32[]{:S(2)}, u32[]{:S(2)}) async-start(f32[16,8,128]{2,1,0:T(8,128)} %broadcast_in_dim.8), calls=%async_computation.6 | async-start | bytes 131072 | tf_op jit(solution)/shard_map/all_to_all | solution.py:324
  141.6 0.0 copy-done.15
  141.7 4.7 %collective-permute-start.4 = (f32[36,128]{1,0:T(8,128)S(1)}, f32[36,128]{1,0:T(8,128)S(1)}, u32[]{:S(2)}, u32[]{:S(2)}) collective-permute-start(f32[36,128]{1,0:T(8,128)S(1)} %copy-done.15), channel_id=1, source_target_pairs={{0,32},{1,33},{2,34},{3,35},{4,36},{5,37},{6,38},{7,39},{8,40},{9,... | collective-permute-start | bytes 55304 | tf_op jit(solution)/shard_map/ppermute | solution.py:394
  146.4 0.0 copy-done.14
  146.4 5.9 %collective-permute-start.5 = (f32[36,128]{1,0:T(8,128)S(1)}, f32[36,128]{1,0:T(8,128)S(1)}, u32[]{:S(2)}, u32[]{:S(2)}) collective-permute-start(f32[36,128]{1,0:T(8,128)S(1)} %copy-done.14), channel_id=1, source_target_pairs={{0,36},{1,37},{2,38},{3,39},{4,40},{5,41},{6,42},{7,43},{8,44},{9,... | collective-permute-start | bytes 55304 | tf_op jit(solution)/shard_map/ppermute | solution.py:394
  152.3 0.0 copy-done.13
  152.3 4.2 %collective-permute-start.6 = (f32[36,128]{1,0:T(8,128)S(1)}, f32[36,128]{1,0:T(8,128)S(1)}, u32[]{:S(2)}, u32[]{:S(2)}) collective-permute-start(f32[36,128]{1,0:T(8,128)S(1)} %copy-done.13), channel_id=1, source_target_pairs={{0,40},{1,41},{2,42},{3,43},{4,44},{5,45},{6,46},{7,47},{8,32},{9,... | collective-permute-start | bytes 55304 | tf_op jit(solution)/shard_map/ppermute | solution.py:394
  156.6 0.0 copy-done.12
  156.6 4.5 %collective-permute-start.7 = (f32[36,128]{1,0:T(8,128)S(1)}, f32[36,128]{1,0:T(8,128)S(1)}, u32[]{:S(2)}, u32[]{:S(2)}) collective-permute-start(f32[36,128]{1,0:T(8,128)S(1)} %copy-done.12), channel_id=1, source_target_pairs={{0,44},{1,45},{2,46},{3,47},{4,32},{5,33},{6,34},{7,35},{8,36},{9,... | collective-permute-start | bytes 55304 | tf_op jit(solution)/shard_map/ppermute | solution.py:394
  161.1 0.0 collective-permute-done.4.refs_0_
  161.2 0.0 copy-start.3
  161.2 0.0 collective-permute-done.5.refs_1_
  161.2 0.0 copy-start.4
  161.2 6.1 %collective-permute-done.6.refs_2_ = f32[36,128]{1,0:T(8,128)S(1)} collective-permute-done((f32[36,128]{1,0:T(8,128)S(1)}, f32[36,128]{1,0:T(8,128)S(1)}, u32[]{:S(2)}, u32[]{:S(2)}) %collective-permute-start.6) | collective-permute-done | bytes 18464 | tf_op jit(solution)/shard_map/ppermute | solution.py:394
  167.3 1.6 collective-permute-done.7.refs_3_
  168.9 0.0 all-to-all-done.6.sums_ref
  168.9 0.0 copy-done.3
  168.9 0.0 copy-done.4
  168.9 0.0 copy-done.5
  168.9 0.6 copy-done.7
  169.5 0.0 copy-done.1
  169.5 2.3 %shard_map.111 = (f32[12,4,384]{2,1,0:T(4,128)}, f32[12,4,384]{2,1,0:T(4,128)}, f32[8,128]{1,0:T(8,128)}) custom-call(s32[1]{0:T(128)} %bitcast.team_ref, f32[16,8,128]{2,1,0:T(8,128)} %copy-done.1, f32[16,12,4,384]{3,2,1,0:T(4,128)} %bitcast.10, f32[12,4,384]{2,1,0:T(4,128)} %get-tuple-element.29.image_ref, f32[12,4,384]{2,1,0:T(4,128)} %bitcast.12, ...), custom_call_target="tpu_custom_call" | custom-call | flops 1000000 | bytes 1500000 | tf_op jit(solution)/shard_map/pallas_call | solution.py:409
  171.8 1.2 slice_bitcast_fusion
  (11 shorter events, 0.1 us)
Async XLA Ops:
  0.6 12.0 %copy-start.16 = (s32[48]{0:T(128)S(1)}, s32[48]{0:T(128)}, u32[]{:S(2)}) copy-start(s32[48]{0:T(128)} %constant.72.clone) | copy-start | bytes 580
  0.6 12.0 %copy-start.11 = (f32[384]{0:T(512)S(1)}, f32[384]{0:T(512)}, u32[]{:S(2)}) copy-start(f32[384]{0:T(512)} %constant.80) | copy-start | bytes 4612
  2.3 19.9 %all-to-all-start = ((f32[4,72,128]{2,1,0:T(8,128)}), f32[4,72,128]{2,1,0:T(8,128)S(1)}, u32[]{:S(2)}, u32[]{:S(2)}) async-start(f32[4,72,128]{2,1,0:T(8,128)} %shard_map.104), calls=%async_computation | async-start | bytes 294912 | tf_op jit(solution)/shard_map/all_to_all | solution.py:360
  22.2 0.7 copy-start.2
  75.0 9.4 %all-to-all-start.4 = ((f32[8,48,128]{2,1,0:T(8,128)}), f32[8,48,128]{2,1,0:T(8,128)S(1)}, u32[]{:S(2)}, u32[]{:S(2)}) async-start(f32[8,48,128]{2,1,0:T(8,128)} %shard_map.108), calls=%async_computation.4 | async-start | bytes 393216 | tf_op jit(solution)/shard_map/all_to_all | solution.py:376
  84.5 0.7 copy-start
  87.5 23.3 %collective-permute-start = (f32[36,128]{1,0:T(8,128)}, f32[36,128]{1,0:T(8,128)S(1)}, u32[]{:S(2)}, u32[]{:S(2)}) collective-permute-start(f32[36,128]{1,0:T(8,128)} %get-tuple-element.24), channel_id=1, source_target_pairs={{0,32},{1,33},{2,34},{3,35},{4,36},{5,37},{6,38},{7,39},{8,40},{9,... | collective-permute-start | bytes 55304 | tf_op jit(solution)/shard_map/ppermute | solution.py:393
  92.0 18.8 %collective-permute-start.1 = (f32[36,128]{1,0:T(8,128)}, f32[36,128]{1,0:T(8,128)S(1)}, u32[]{:S(2)}, u32[]{:S(2)}) collective-permute-start(f32[36,128]{1,0:T(8,128)} %get-tuple-element.25), channel_id=1, source_target_pairs={{0,36},{1,37},{2,38},{3,39},{4,40},{5,41},{6,42},{7,43},{8,44},{9,... | collective-permute-start | bytes 55304 | tf_op jit(solution)/shard_map/ppermute | solution.py:393
  97.3 14.9 %collective-permute-start.2 = (f32[36,128]{1,0:T(8,128)}, f32[36,128]{1,0:T(8,128)S(1)}, u32[]{:S(2)}, u32[]{:S(2)}) collective-permute-start(f32[36,128]{1,0:T(8,128)} %get-tuple-element.26), channel_id=1, source_target_pairs={{0,40},{1,41},{2,42},{3,43},{4,44},{5,45},{6,46},{7,47},{8,32},{9,... | collective-permute-start | bytes 55304 | tf_op jit(solution)/shard_map/ppermute | solution.py:393
  102.0 12.7 %collective-permute-start.3 = (f32[36,128]{1,0:T(8,128)}, f32[36,128]{1,0:T(8,128)S(1)}, u32[]{:S(2)}, u32[]{:S(2)}) collective-permute-start(f32[36,128]{1,0:T(8,128)} %get-tuple-element.27), channel_id=1, source_target_pairs={{0,44},{1,45},{2,46},{3,47},{4,32},{5,33},{6,34},{7,35},{8,36},{9,... | collective-permute-start | bytes 55304 | tf_op jit(solution)/shard_map/ppermute | solution.py:393
  110.8 30.9 %copy-start.15 = (f32[36,128]{1,0:T(8,128)S(1)}, f32[36,128]{1,0:T(8,128)}, u32[]{:S(2)}) copy-start(f32[36,128]{1,0:T(8,128)} %get-tuple-element.30) | copy-start | bytes 55300
  110.8 35.6 %copy-start.14 = (f32[36,128]{1,0:T(8,128)S(1)}, f32[36,128]{1,0:T(8,128)}, u32[]{:S(2)}) copy-start(f32[36,128]{1,0:T(8,128)} %get-tuple-element.31) | copy-start | bytes 55300
  110.8 41.6 %copy-start.13 = (f32[36,128]{1,0:T(8,128)S(1)}, f32[36,128]{1,0:T(8,128)}, u32[]{:S(2)}) copy-start(f32[36,128]{1,0:T(8,128)} %get-tuple-element.32) | copy-start | bytes 55300
  110.8 45.8 %copy-start.12 = (f32[36,128]{1,0:T(8,128)S(1)}, f32[36,128]{1,0:T(8,128)}, u32[]{:S(2)}) copy-start(f32[36,128]{1,0:T(8,128)} %get-tuple-element.33) | copy-start | bytes 55300
  110.8 4.0 %copy-start.6 = (f32[36,128]{1,0:T(8,128)}, f32[36,128]{1,0:T(8,128)S(1)}, u32[]{:S(2)}) copy-start(f32[36,128]{1,0:T(8,128)S(1)} %collective-permute-done.refs_0_) | copy-start | bytes 55300
  110.8 3.9 %copy-start.8 = (f32[36,128]{1,0:T(8,128)}, f32[36,128]{1,0:T(8,128)S(1)}, u32[]{:S(2)}) copy-start(f32[36,128]{1,0:T(8,128)S(1)} %collective-permute-done.1.refs_1_) | copy-start | bytes 55300
  112.2 2.5 %copy-start.9 = (f32[36,128]{1,0:T(8,128)}, f32[36,128]{1,0:T(8,128)S(1)}, u32[]{:S(2)}) copy-start(f32[36,128]{1,0:T(8,128)S(1)} %collective-permute-done.2.refs_2_) | copy-start | bytes 55300
  114.7 0.6 copy-start.10
  135.0 33.9 %all-to-all-start.6 = ((f32[16,8,128]{2,1,0:T(8,128)}), f32[16,8,128]{2,1,0:T(8,128)S(1)}, u32[]{:S(2)}, u32[]{:S(2)}) async-start(f32[16,8,128]{2,1,0:T(8,128)} %broadcast_in_dim.8), calls=%async_computation.6 | async-start | bytes 131072 | tf_op jit(solution)/shard_map/all_to_all | solution.py:324
  141.7 19.5 %collective-permute-start.4 = (f32[36,128]{1,0:T(8,128)S(1)}, f32[36,128]{1,0:T(8,128)S(1)}, u32[]{:S(2)}, u32[]{:S(2)}) collective-permute-start(f32[36,128]{1,0:T(8,128)S(1)} %copy-done.15), channel_id=1, source_target_pairs={{0,32},{1,33},{2,34},{3,35},{4,36},{5,37},{6,38},{7,39},{8,40},{9,... | collective-permute-start | bytes 55304 | tf_op jit(solution)/shard_map/ppermute | solution.py:394
  146.4 14.8 %collective-permute-start.5 = (f32[36,128]{1,0:T(8,128)S(1)}, f32[36,128]{1,0:T(8,128)S(1)}, u32[]{:S(2)}, u32[]{:S(2)}) collective-permute-start(f32[36,128]{1,0:T(8,128)S(1)} %copy-done.14), channel_id=1, source_target_pairs={{0,36},{1,37},{2,38},{3,39},{4,40},{5,41},{6,42},{7,43},{8,44},{9,... | collective-permute-start | bytes 55304 | tf_op jit(solution)/shard_map/ppermute | solution.py:394
  152.3 14.9 %collective-permute-start.6 = (f32[36,128]{1,0:T(8,128)S(1)}, f32[36,128]{1,0:T(8,128)S(1)}, u32[]{:S(2)}, u32[]{:S(2)}) collective-permute-start(f32[36,128]{1,0:T(8,128)S(1)} %copy-done.13), channel_id=1, source_target_pairs={{0,40},{1,41},{2,42},{3,43},{4,44},{5,45},{6,46},{7,47},{8,32},{9,... | collective-permute-start | bytes 55304 | tf_op jit(solution)/shard_map/ppermute | solution.py:394
  156.6 12.3 %collective-permute-start.7 = (f32[36,128]{1,0:T(8,128)S(1)}, f32[36,128]{1,0:T(8,128)S(1)}, u32[]{:S(2)}, u32[]{:S(2)}) collective-permute-start(f32[36,128]{1,0:T(8,128)S(1)} %copy-done.12), channel_id=1, source_target_pairs={{0,44},{1,45},{2,46},{3,47},{4,32},{5,33},{6,34},{7,35},{8,36},{9,... | collective-permute-start | bytes 55304 | tf_op jit(solution)/shard_map/ppermute | solution.py:394
  161.2 7.7 %copy-start.3 = (f32[36,128]{1,0:T(8,128)}, f32[36,128]{1,0:T(8,128)S(1)}, u32[]{:S(2)}) copy-start(f32[36,128]{1,0:T(8,128)S(1)} %collective-permute-done.4.refs_0_) | copy-start | bytes 55300
  161.2 7.7 %copy-start.4 = (f32[36,128]{1,0:T(8,128)}, f32[36,128]{1,0:T(8,128)S(1)}, u32[]{:S(2)}) copy-start(f32[36,128]{1,0:T(8,128)S(1)} %collective-permute-done.5.refs_1_) | copy-start | bytes 55300
  167.3 1.6 copy-start.5
  168.9 0.6 copy-start.7
  168.9 0.6 copy-start.1

commit v2 on v1

--- a/solution.py
+++ b/solution.py
@@ -91,14 +91,24 @@
     return both[0:NX] + both[NX : 2 * NX] + mm(table_ref[0:NX, :], low)
 
 
-def call(kernel, outs, scratch=(), flops=0, moved=0):
-    return pl.pallas_call(
+def call(kernel, outs, operands, scratch=(), flops=0, moved=0, keep=True):
+    vmem = pl.BlockSpec(memory_space=pltpu.VMEM)
+    single = not isinstance(outs, (list, tuple))
+    shapes = [outs] if single else list(outs)
+    if not INTERPRET:
+        operands = [pltpu.with_memory_space_constraint(x, pltpu.VMEM) for x in operands]
+        shapes = [pltpu.VMEM(x.shape, x.dtype) for x in shapes] if keep else shapes
+    results = pl.pallas_call(
         kernel,
-        out_shape=outs,
+        in_specs=[vmem] * len(operands),
+        out_specs=[vmem] * len(shapes),
+        out_shape=shapes,
         scratch_shapes=list(scratch),
         cost_estimate=pl.CostEstimate(flops=flops, bytes_accessed=moved, transcendentals=0),
+        compiler_params=pltpu.CompilerParams(vmem_limit_bytes=24 << 20),
         interpret=INTERPRET,
-    )
+    )(*operands)
+    return results[0] if single else results
 
 
 def f32(*shape):
@@ -194,18 +204,15 @@
     spread(fields, inverse_ref, cas_ref, slope_ref, send_ref)
 
 
-def last_kernel(team_ref, recv_ref, old_ref, damping_ref, cas_ref, *refs):
-    outs, keep = refs[:8], refs[8]
+def last_kernel(recv_ref, old_ref, damping_ref, cas_ref, out_ref):
     fields = advanced(recv_ref, old_ref, damping_ref, cas_ref)
     for member in range(2):
         for q in range(4):
             for t in range(3):
-                keep[member, q, CUT * t : CUT * (t + 1), :] = fields[member][
+                row = 36 * member + CUT * t
+                out_ref[q, row : row + CUT, :] = fields[member][
                     CUT * q : CUT * (q + 1), tile(t)
                 ]
-    for member in range(2):
-        for d in range(4):
-            outs[4 * member + d][...] = keep[member, lax.rem(team_ref[0] + d, 4)]
 
 
 def row_sums(value):
@@ -255,17 +262,14 @@
     )
 
 
-def place(team_ref, parts, out_ref, order):
-    for d in range(4):
-        order[lax.rem(team_ref[0] + 4 - d, 4)] = parts[d][...]
+def place(planes_ref, out_ref):
     for p in range(PLANES):
         for t in range(3):
-            out_ref[:, p, tile(t)] = order[p, CUT * t : CUT * (t + 1), :]
-
-
-def dots_kernel(team_ref, kry_ref, gram_ref, *refs):
-    parts, image_ref, out_ref, keep, order = refs[:4], refs[4], refs[5], refs[6], refs[7]
-    place(team_ref, parts, image_ref, order)
+            out_ref[:, p, tile(t)] = planes_ref[p, CUT * t : CUT * (t + 1), :]
+
+
+def dots_kernel(planes_ref, kry_ref, gram_ref, image_ref, out_ref, keep):
+    place(planes_ref, image_ref)
     image = image_ref[...] - kry_ref[KRY - 1]
     image_ref[...] = image
     keep[...] = jnp.zeros_like(keep)
@@ -274,12 +278,15 @@
     keep[KRY : KRY + 1, :] = fold(jnp.sum(image * image, axis=0))
     packed = row_sums(keep[...])
     row = lax.broadcasted_iota(jnp.int32, (8, TILE), 0)
-    out_ref[...] = jnp.where(row == 0, packed, gram_ref[...])
-
-
-def finish_kernel(team_ref, sums_ref, kry_ref, image_ref, state_ref, *refs):
-    parts, residual_ref, next_ref, hess_ref, order = refs[:4], refs[4], refs[5], refs[6], refs[7]
-    place(team_ref, parts, residual_ref, order)
+    sums = jnp.where(row == 0, packed, gram_ref[...])
+    for m in range(out_ref.shape[0]):
+        out_ref[m] = sums
+
+
+def finish_kernel(
+    sums_ref, kry_ref, image_ref, state_ref, planes_ref, residual_ref, next_ref, hess_ref
+):
+    place(planes_ref, residual_ref)
     residual_ref[...] = residual_ref[...] - state_ref[...]
     total = float(SEGS * PLANES * NZ * NX)
     sums = sums_ref[0]
@@ -303,31 +310,12 @@
     norm = jnp.sqrt(jnp.maximum(squared, 0.0) + 1e-06)
     next_ref[...] = remain / norm
     hess = jnp.where(lane == KRY, norm, sums[0:1])
-    hess_ref[...] = jnp.broadcast_to(hess, (8, TILE))
-
-
-def route(distance, segs):
-    pairs = []
-    for s in range(segs):
-        for y in range(2):
-            for q in range(4):
-                for r in range(4):
-                    here = s * PEN + pen_index(y, q, r)
-                    there = (s + 1) % segs * PEN + pen_index(y, (q + distance) % 4, r)
-                    pairs.append((here, there))
-    return pairs
-
-
-def gathered(value, axis):
-    size = lax.axis_size(axis)
-    copies = jnp.broadcast_to(value[None], (size,) + value.shape)
-    return lax.all_to_all(copies, axis, 0, 0, tiled=True)
+    hess_ref[...] = hess[0, : KRY + 1]
 
 
 def body(state, krylov):
     pen = lax.axis_index("pen")
     segs = lax.axis_size("seg")
-    team = (pen // 4) % 4
     numbers = np.arange(NX)
     signed = np.where(numbers <= NX // 2, numbers, numbers - NX).astype(np.float32)
     steps = np.arange(WIDE)
@@ -337,85 +325,89 @@
     inverse = jnp.where(ksquare > 0, 1.0 / jnp.where(ksquare > 0, ksquare, 1.0), 0.0)
     damping = 1.0 / (1.0 + time_step * viscosity * ksquare)
     cas, slope, cas_z, slope_z = [jnp.asarray(t) for t in tables()]
-    team_ref = team.astype(jnp.int32).reshape(1)
-    smem = pl.BlockSpec(memory_space=pltpu.SMEM)
-    vmem = pl.BlockSpec(memory_space=pltpu.VMEM)
-
     state_f = state.transpose(1, 0, 2)
     kry_f = krylov.transpose(0, 2, 1, 3)
     exchange = functools.partial(
         lax.all_to_all, axis_name="pen", split_axis=0, concat_axis=0, tiled=True
     )
+    ring = [(s, (s + 1) % segs) for s in range(segs)]
 
     whole = pl.BlockSpec((CUT, PLANES, NX), lambda i: (0, 0, 0))
     last = pl.BlockSpec((None, CUT, PLANES, NX), lambda i: (KRY - 1, 0, 0, 0))
+    inputs = [state_f, kry_f]
+    if not INTERPRET:
+        inputs = [pltpu.with_memory_space_constraint(x, pltpu.HBM) for x in inputs]
     packed = pl.pallas_call(
         gather_rows,
         grid=(1,),
         in_specs=[whole, last],
         out_specs=pl.BlockSpec((4, 72, TILE), lambda i: (0, 0, 0)),
         out_shape=f32(4, 72, TILE),
+        compiler_params=pltpu.CompilerParams(vmem_limit_bytes=24 << 20),
         interpret=INTERPRET,
-    )(state_f, kry_f)
+    )(*inputs)
     packed = exchange(packed, axis_index_groups=PEERS)
     gram = call(
         gram_kernel,
         f32(8, TILE),
+        [kry_f],
         [pltpu.VMEM((KRY * KRY, TILE), jnp.float32)],
         flops=10_000_000,
         moved=1_300_000,
-    )(kry_f)
+    )
+    packed, gram = lax.optimization_barrier((packed, gram))
+    both = (f32(TEAM, 144, TILE), f32(2, WIDE, NX))
     send, fields = call(
-        first_kernel, (f32(TEAM, 144, TILE), f32(2, WIDE, NX)), flops=700_000_000, moved=3_000_000
-    )(packed, inverse, cas, slope)
+        first_kernel, both, [packed, inverse, cas, slope], flops=700_000_000, moved=3_000_000
+    )
     for repeat in range(STEPS):
         recv = exchange(send, axis_index_groups=TEAMS)
         modes = call(
-            grid_kernel, f32(TEAM, WIDE, TILE), flops=900_000_000, moved=2_500_000
-        )(recv, cas_z, slope_z)
+            grid_kernel,
+            f32(TEAM, WIDE, TILE),
+            [recv, cas_z, slope_z],
+            flops=900_000_000,
+            moved=2_500_000,
+        )
         recv = exchange(modes, axis_index_groups=TEAMS)
         if repeat < STEPS - 1:
             send, fields = call(
                 middle_kernel,
-                (f32(TEAM, 144, TILE), f32(2, WIDE, NX)),
+                both,
+                [recv, fields, damping, inverse, cas, slope],
                 flops=900_000_000,
                 moved=3_000_000,
-            )(recv, fields, damping, inverse, cas, slope)
-    pieces = pl.pallas_call(
+            )
+    ends = call(
         last_kernel,
-        in_specs=[smem] + [vmem] * 4,
-        out_specs=[vmem] * 8,
-        out_shape=[f32(36, TILE)] * 8,
-        scratch_shapes=[pltpu.VMEM((2, 4, 36, TILE), jnp.float32)],
-        cost_estimate=pl.CostEstimate(flops=200_000_000, bytes_accessed=1_500_000, transcendentals=0),
-        interpret=INTERPRET,
-    )(team_ref, recv, fields, damping, cas)
-    tangent = [lax.ppermute(pieces[4 + d], ("seg", "pen"), route(d, segs)) for d in range(4)]
-    base = [lax.ppermute(pieces[d], ("seg", "pen"), route(d, segs)) for d in range(4)]
-    image, partial = pl.pallas_call(
+        f32(4, 72, TILE),
+        [recv, fields, damping, cas],
+        flops=200_000_000,
+        moved=1_500_000,
+    )
+    ends = exchange(ends, axis_index_groups=PEERS)
+    tangent = lax.ppermute(ends[:, 36:72], "seg", ring)
+    base = lax.ppermute(ends[:, 0:36], "seg", ring)
+    image, partial = call(
         dots_kernel,
-        in_specs=[smem] + [vmem] * 6,
-        out_specs=[vmem] * 2,
-        out_shape=[f32(CUT, PLANES, NX), f32(8, TILE)],
-        scratch_shapes=[
-            pltpu.VMEM((TILE, TILE), jnp.float32),
-            pltpu.VMEM((4, 36, TILE), jnp.float32),
-        ],
-        cost_estimate=pl.CostEstimate(flops=1_000_000, bytes_accessed=1_300_000, transcendentals=0),
-        interpret=INTERPRET,
-    )(team_ref, kry_f, gram, *tangent)
-    sums = gathered(partial, "pen")
-    sums = gathered(jnp.sum(sums, axis=0), "seg")
-    residual, vector, hess = pl.pallas_call(
+        [f32(CUT, PLANES, NX), f32(PEN, 8, TILE)],
+        [tangent, kry_f, gram],
+        [pltpu.VMEM((TILE, TILE), jnp.float32)],
+        flops=1_000_000,
+        moved=1_300_000,
+    )
+    sums = jnp.sum(exchange(partial), axis=0)
+    sums = jnp.broadcast_to(sums[None], (segs, 8, TILE))
+    sums = lax.all_to_all(sums, "seg", 0, 0, tiled=True)
+    residual, vector, hess = call(
         finish_kernel,
-        in_specs=[smem] + [vmem] * 8,
-        out_specs=[vmem] * 3,
-        out_shape=[f32(CUT, PLANES, NX)] * 2 + [f32(8, TILE)],
-        scratch_shapes=[pltpu.VMEM((4, 36, TILE), jnp.float32)],
-        cost_estimate=pl.CostEstimate(flops=1_000_000, bytes_accessed=1_500_000, transcendentals=0),
-        interpret=INTERPRET,
-    )(team_ref, sums, kry_f, image, state_f, *base)
-    return (residual.transpose(1, 0, 2), vector.transpose(1, 0, 2), hess[0, : KRY + 1])
+        [f32(CUT, PLANES, NX)] * 2 + [f32(KRY + 1)],
+        [sums, kry_f, image, state_f, base],
+        flops=1_000_000,
+        moved=1_500_000,
+        keep=False,
+    )
+    return (residual.transpose(1, 0, 2), vector.transpose(1, 0, 2), hess)
 
 
 def solution(mesh):

time: 174 us -> 129 us (0.74)
  starting transfers between devices: 60.1 us -> 27.1 us
  Pallas kernels: 27.4 us -> 11.7 us
  blocking collectives: 53.6 us -> 66.7 us
  waiting for transfers between devices: 25.2 us -> 20.8 us
  local copies, waits for them, and re-layouts: 5.09 us -> 0.7 us
    ppermute x8 -> x2, starting transfers between devices: 38.4 us -> 9.22 us  [the longest x1 4.72 us: body(): base = lax.ppermute(ends[:, 0:36], 'seg', ring)]
    pallas_call x8, Pallas kernels: 25.7 us -> 9.97 us  [call(): pl.pallas_call(kernel, in_specs=[vmem] * len(operands), out_specs=[vmem]...]
    all_to_all x1 -> x2, blocking collectives: 15.8 us -> 25.2 us  [the longest x1 13.3 us: body(): sums = jnp.sum(exchange(partial), axis=0)]
    all_to_all x1 -> x2, blocking collectives: 10.1 us -> 17 us  [body(): recv = exchange(modes, axis_index_groups=TEAMS)]
    all_to_all x2 -> x1, waiting for transfers between devices: 4.76 us -> 0.01 us  [body(): sums = lax.all_to_all(sums, 'seg', 0, 0, tiled=True)]
    all_to_all x2 -> x1, starting transfers between devices: 11.3 us -> 7.46 us  [body(): sums = lax.all_to_all(sums, 'seg', 0, 0, tiled=True)]
    all_to_all x2, blocking collectives: 27.6 us -> 24.5 us  [body(): recv = exchange(send, axis_index_groups=TEAMS)]
    unnamed x34 -> x16, local copies, waits for them, and re-layouts: 2.58 us -> 0.05 us
  transfers between devices with their start and end apart: 11 -> 4, of which waited for: 6 -> 3; matrix products, arithmetic and copies ran while one was open for 0% -> 0% of each run, Pallas kernels for 2% -> 2%
where the time goes in v2:
time: 129 us; the launch traced here: 128 us
  blocking collectives  66.7 us (52%)
  starting transfers between devices  27.1 us (21%)
  waiting for transfers between devices  20.8 us (16%)
  Pallas kernels  11.7 us (9%)
    all_to_all x2, blocking collectives, body(): recv = exchange(send, axis_index_groups=TEAMS)  24.5 us
    all_to_all x2, blocking collectives, body(): recv = exchange(modes, axis_index_groups=TEAMS)  17 us
    all_to_all x1, blocking collectives, body(): sums = jnp.sum(exchange(partial), axis=0)  13.3 us
    all_to_all x1, blocking collectives, body(): ends = exchange(ends, axis_index_groups=PEERS)  11.9 us
    all_to_all x1, starting transfers between devices, body(): packed = exchange(packed, axis_index_groups=PEERS)  10.4 us
    pallas_call x8, Pallas kernels, call(): pl.pallas_call(kernel, in_specs=[vmem] * len(operands), out_specs=[vmem]...  9.97 us
    ppermute x1, waiting for transfers between devices, body(): base = lax.ppermute(ends[:, 0:36], 'seg', ring)  7.52 us
    all_to_all x1, starting transfers between devices, body(): sums = lax.all_to_all(sums, 'seg', 0, 0, tiled=True)  7.46 us
  transfers between devices with their start and end apart: 4, of which 3 were waited for; matrix products, arithmetic and copies ran while one was open for 0% of the time, Pallas kernels for 2%

profile of v2, /device:TPU:8, one launch (start us, length us, event | category | flops | bytes accessed | tf_op | source)
XLA Modules:
  0.0 128.0 jit_solution(15674448745166915991)
XLA Ops:
  0.6 0.0 copy-start
  0.6 0.0 copy-start.7
  0.7 0.0 copy-start.6
  0.7 1.8 %shard_map.103 = f32[4,72,128]{2,1,0:T(8,128)} custom-call(f32[12,4,384]{2,1,0:T(4,128)} %bitcast.8, f32[16,12,4,384]{3,2,1,0:T(4,128)} %bitcast.4), custom_call_target="tpu_custom_call" | custom-call | tf_op jit(solution)/shard_map/pallas_call | solution.py:340
  2.4 0.0 copy-start.1
  2.4 0.0 copy-start.5
  2.4 10.4 %all-to-all-start = ((f32[4,72,128]{2,1,0:T(8,128)}), f32[4,72,128]{2,1,0:T(8,128)S(1)}, u32[]{:S(2)}, u32[]{:S(2)}) async-start(f32[4,72,128]{2,1,0:T(8,128)} %shard_map.103), calls=%async_computation | async-start | bytes 294912 | tf_op jit(solution)/shard_map/all_to_all | solution.py:349
  12.9 0.0 copy-done
  12.9 2.3 %shard_map.104.gram_ref = f32[8,128]{1,0:T(8,128)S(1)} custom-call(f32[16,12,4,384]{3,2,1,0:T(4,128)S(1)} %bitcast.5), custom_call_target="tpu_custom_call" | custom-call | flops 10000000 | bytes 1300000 | tf_op jit(solution)/shard_map/pallas_call | solution.py:101
  15.2 0.0 copy-done.7
  15.2 0.1 fusion.5
  15.3 0.0 copy-done.6
  15.3 0.1 fusion.3
  15.4 7.1 %all-to-all-done.recv_ref = f32[4,72,128]{2,1,0:T(8,128)S(1)} async-done(((f32[4,72,128]{2,1,0:T(8,128)}), f32[4,72,128]{2,1,0:T(8,128)S(1)}, u32[]{:S(2)}, u32[]{:S(2)}) %all-to-all-start) | async-done | bytes 147488 | tf_op jit(solution)/shard_map/all_to_all | solution.py:349
  22.5 0.0 copy-done.1
  22.5 0.0 copy-done.5
  22.5 1.0 shard_map.105
  23.4 0.0 copy-start.3
  23.4 0.0 copy-start.4
  23.5 12.2 %all_to_all.40.recv_ref = f32[8,144,128]{2,1,0:T(8,128)S(1)} all-to-all(f32[8,144,128]{2,1,0:T(8,128)S(1)} %get-tuple-element.15), channel_id=1, replica_groups={{0,1,2,3,16,17,18,19},{4,5,6,7,20,21,22,23},{8,9,10,11,24,25,26,27},{12..., dimensions={0} | all-to-all | bytes 1179648 | tf_op jit(solution)/shard_map/all_to_all | solution.py:364
  35.6 0.0 copy-done.3
  35.6 0.0 copy-done.4
  35.6 1.7 %shard_map.106 = f32[8,48,128]{2,1,0:T(8,128)S(1)} custom-call(f32[8,144,128]{2,1,0:T(8,128)S(1)} %all_to_all.40.recv_ref, bf16[768,384]{1,0:T(8,128)(2,1)S(1)} %copy-done.4, bf16[768,384]{1,0:T(8,128)(2,1)S(1)} %copy-done.3), custom_call_target="tpu_custom_call" | custom-call | flops 900000000 | bytes 2500000 | tf_op jit(solution)/shard_map/pallas_call | solution.py:101
  37.4 8.5 %all_to_all.41.recv_ref = f32[8,48,128]{2,1,0:T(8,128)S(1)} all-to-all(f32[8,48,128]{2,1,0:T(8,128)S(1)} %shard_map.106), channel_id=1, replica_groups={{0,1,2,3,16,17,18,19},{4,5,6,7,20,21,22,23},{8,9,10,11,24,25,26,27},{12..., dimensions={0} | all-to-all | bytes 393216 | tf_op jit(solution)/shard_map/all_to_all | solution.py:372
  45.9 1.3 %shard_map.107 = (f32[8,144,128]{2,1,0:T(8,128)S(1)}, f32[2,48,384]{2,1,0:T(8,128)S(1)}) custom-call(f32[8,48,128]{2,1,0:T(8,128)S(1)} %all_to_all.41.recv_ref, f32[2,48,384]{2,1,0:T(8,128)S(1)} %get-tuple-element.16.old_ref, f32[48,384]{1,0:T(8,128)S(1)} %get-tuple-element.27.damping_ref, f32[48,384]{1,0:T(8,128)S(1)} %get-tuple-element.28.inverse_ref, ...), custom_call_target="tpu_custom_call" | custom-call | flops 900000000 | bytes 3000000 | tf_op jit(solution)/shard_map/pallas_call | solution.py:101
  47.2 12.3 %all_to_all.42.recv_ref = f32[8,144,128]{2,1,0:T(8,128)S(1)} all-to-all(f32[8,144,128]{2,1,0:T(8,128)S(1)} %get-tuple-element.17), channel_id=1, replica_groups={{0,1,2,3,16,17,18,19},{4,5,6,7,20,21,22,23},{8,9,10,11,24,25,26,27},{12..., dimensions={0} | all-to-all | bytes 1179648 | tf_op jit(solution)/shard_map/all_to_all | solution.py:364
  59.5 1.7 %shard_map.108 = f32[8,48,128]{2,1,0:T(8,128)S(1)} custom-call(f32[8,144,128]{2,1,0:T(8,128)S(1)} %all_to_all.42.recv_ref, bf16[768,384]{1,0:T(8,128)(2,1)S(1)} %copy-done.4, bf16[768,384]{1,0:T(8,128)(2,1)S(1)} %copy-done.3), custom_call_target="tpu_custom_call" | custom-call | flops 900000000 | bytes 2500000 | tf_op jit(solution)/shard_map/pallas_call | solution.py:101
  61.2 8.5 %all_to_all.43.recv_ref = f32[8,48,128]{2,1,0:T(8,128)S(1)} all-to-all(f32[8,48,128]{2,1,0:T(8,128)S(1)} %shard_map.108), channel_id=1, replica_groups={{0,1,2,3,16,17,18,19},{4,5,6,7,20,21,22,23},{8,9,10,11,24,25,26,27},{12..., dimensions={0} | all-to-all | bytes 393216 | tf_op jit(solution)/shard_map/all_to_all | solution.py:372
  69.8 0.4 shard_map.109
  70.1 0.0 copy-start.2
  70.2 11.9 %all_to_all.44 = f32[4,72,128]{2,1,0:T(8,128)S(1)} all-to-all(f32[4,72,128]{2,1,0:T(8,128)S(1)} %shard_map.109), channel_id=1, replica_groups={{0,4,8,12},{1,5,9,13},{2,6,10,14},{3,7,11,15},{16,20,24,28},{17,21,25,2..., dimensions={0} | all-to-all | bytes 294912 | tf_op jit(solution)/shard_map/all_to_all | solution.py:388
  82.1 4.5 %collective-permute-start = (f32[4,36,128]{2,1,0:T(8,128)S(1)}, f32[4,36,128]{2,1,0:T(8,128)S(1)}, u32[]{:S(2)}, u32[]{:S(2)}) collective-permute-start(f32[4,36,128]{2,1,0:T(8,128)S(1)} %get-tuple-element.26), channel_id=1, source_target_pairs={{0,32},{32,64},{64,96},{96,128},{128,160},{160,192},{192,224},{224... | collective-permute-start | bytes 221192 | tf_op jit(solution)/shard_map/ppermute | solution.py:389
  86.6 6.2 %collective-permute-done.planes_ref = f32[4,36,128]{2,1,0:T(8,128)S(1)} collective-permute-done((f32[4,36,128]{2,1,0:T(8,128)S(1)}, f32[4,36,128]{2,1,0:T(8,128)S(1)}, u32[]{:S(2)}, u32[]{:S(2)}) %collective-permute-start) | collective-permute-done | bytes 73760 | tf_op jit(solution)/shard_map/ppermute | solution.py:389
  92.7 0.5 shard_map.110
  93.3 13.3 %all_to_all.45 = f32[32,8,128]{2,1,0:T(8,128)S(1)} all-to-all(f32[32,8,128]{2,1,0:T(8,128)S(1)} %get-tuple-element.20), channel_id=1, replica_groups=mesh['seg'=16,'pen'=32] {'pen'}, dimensions={0} | all-to-all | bytes 262144 | tf_op jit(solution)/shard_map/all_to_all | solution.py:399
  106.6 0.6 broadcast_in_dim.5
  107.2 7.5 %all-to-all-start.7 = ((f32[16,8,128]{2,1,0:T(8,128)}), f32[16,8,128]{2,1,0:T(8,128)S(1)}, u32[]{:S(2)}, u32[]{:S(2)}) async-start(f32[16,8,128]{2,1,0:T(8,128)} %broadcast_in_dim.5), calls=%async_computation.7 | async-start | bytes 131072 | tf_op jit(solution)/shard_map/all_to_all | solution.py:401
  114.7 4.7 %collective-permute-start.1 = (f32[4,36,128]{2,1,0:T(8,128)S(1)}, f32[4,36,128]{2,1,0:T(8,128)S(1)}, u32[]{:S(2)}, u32[]{:S(2)}) collective-permute-start(f32[4,36,128]{2,1,0:T(8,128)S(1)} %get-tuple-element.25), channel_id=1, source_target_pairs={{0,32},{32,64},{64,96},{96,128},{128,160},{160,192},{192,224},{224... | collective-permute-start | bytes 221192 | tf_op jit(solution)/shard_map/ppermute | solution.py:390
  119.4 7.5 %collective-permute-done.1.planes_ref = f32[4,36,128]{2,1,0:T(8,128)S(1)} collective-permute-done((f32[4,36,128]{2,1,0:T(8,128)S(1)}, f32[4,36,128]{2,1,0:T(8,128)S(1)}, u32[]{:S(2)}, u32[]{:S(2)}) %collective-permute-start.1) | collective-permute-done | bytes 73760 | tf_op jit(solution)/shard_map/ppermute | solution.py:390
  127.0 0.0 all-to-all-done.7.sums_ref
  127.0 0.0 copy-done.2
  127.0 1.0 shard_map.111
  (2 shorter events, 0.0 us)
Async XLA Ops:
  0.6 12.2 %copy-start = (f32[16,4,12,384]{3,1,2,0:T(4,128)S(1)}, f32[16,4,12,384]{3,1,2,0:T(4,128)}, u32[]{:S(2)}) copy-start(f32[16,4,12,384]{3,1,2,0:T(4,128)} %param.9) | copy-start | bytes 3538948
  0.6 14.5 %copy-start.7 = (s32[48]{0:T(128)S(1)}, s32[48]{0:T(128)}, u32[]{:S(2)}) copy-start(s32[48]{0:T(128)} %constant.59.clone) | copy-start | bytes 580
  0.7 14.6 %copy-start.6 = (f32[384]{0:T(512)S(1)}, f32[384]{0:T(512)}, u32[]{:S(2)}) copy-start(f32[384]{0:T(512)} %constant.67) | copy-start | bytes 4612
  2.4 20.0 %copy-start.1 = (bf16[768,384]{1,0:T(8,128)(2,1)S(1)}, bf16[768,384]{1,0:T(8,128)(2,1)}, u32[]{:S(2)}) copy-start(bf16[768,384]{1,0:T(8,128)(2,1)} %constant.61.clone.cas_ref) | copy-start | bytes 1769476
  2.4 20.0 %copy-start.5 = (bf16[768,384]{1,0:T(8,128)(2,1)S(1)}, bf16[768,384]{1,0:T(8,128)(2,1)}, u32[]{:S(2)}) copy-start(bf16[768,384]{1,0:T(8,128)(2,1)} %constant.62.clone.slope_ref) | copy-start | bytes 1769476
  2.4 20.0 %all-to-all-start = ((f32[4,72,128]{2,1,0:T(8,128)}), f32[4,72,128]{2,1,0:T(8,128)S(1)}, u32[]{:S(2)}, u32[]{:S(2)}) async-start(f32[4,72,128]{2,1,0:T(8,128)} %shard_map.103), calls=%async_computation | async-start | bytes 294912 | tf_op jit(solution)/shard_map/all_to_all | solution.py:349
  23.4 12.2 %copy-start.3 = (bf16[768,384]{1,0:T(8,128)(2,1)S(1)}, bf16[768,384]{1,0:T(8,128)(2,1)}, u32[]{:S(2)}) copy-start(bf16[768,384]{1,0:T(8,128)(2,1)} %constant.64.clone.slope_ref) | copy-start | bytes 1769476
  23.4 12.2 %copy-start.4 = (bf16[768,384]{1,0:T(8,128)(2,1)S(1)}, bf16[768,384]{1,0:T(8,128)(2,1)}, u32[]{:S(2)}) copy-start(bf16[768,384]{1,0:T(8,128)(2,1)} %constant.63.clone.cas_ref) | copy-start | bytes 1769476
  70.1 56.8 %copy-start.2 = (f32[4,12,384]{2,0,1:T(4,128)S(1)}, f32[4,12,384]{2,0,1:T(4,128)}, u32[]{:S(2)}) copy-start(f32[4,12,384]{2,0,1:T(4,128)} %param.8) | copy-start | bytes 221188
  82.1 10.7 %collective-permute-start = (f32[4,36,128]{2,1,0:T(8,128)S(1)}, f32[4,36,128]{2,1,0:T(8,128)S(1)}, u32[]{:S(2)}, u32[]{:S(2)}) collective-permute-start(f32[4,36,128]{2,1,0:T(8,128)S(1)} %get-tuple-element.26), channel_id=1, source_target_pairs={{0,32},{32,64},{64,96},{96,128},{128,160},{160,192},{192,224},{224... | collective-permute-start | bytes 221192 | tf_op jit(solution)/shard_map/ppermute | solution.py:389
  107.2 19.7 %all-to-all-start.7 = ((f32[16,8,128]{2,1,0:T(8,128)}), f32[16,8,128]{2,1,0:T(8,128)S(1)}, u32[]{:S(2)}, u32[]{:S(2)}) async-start(f32[16,8,128]{2,1,0:T(8,128)} %broadcast_in_dim.5), calls=%async_computation.7 | async-start | bytes 131072 | tf_op jit(solution)/shard_map/all_to_all | solution.py:401
  114.7 12.3 %collective-permute-start.1 = (f32[4,36,128]{2,1,0:T(8,128)S(1)}, f32[4,36,128]{2,1,0:T(8,128)S(1)}, u32[]{:S(2)}, u32[]{:S(2)}) collective-permute-start(f32[4,36,128]{2,1,0:T(8,128)S(1)} %get-tuple-element.25), channel_id=1, source_target_pairs={{0,32},{32,64},{64,96},{96,128},{128,160},{160,192},{192,224},{224... | collective-permute-start | bytes 221192 | tf_op jit(solution)/shard_map/ppermute | solution.py:390

commit v3 on v2

--- a/solution.py
+++ b/solution.py
@@ -7,6 +7,7 @@
 from jax.experimental import pallas as pl
 from jax.experimental.pallas import tpu as pltpu
 from jax.sharding import PartitionSpec as P
+
 
 NX = 384
 NZ = 384
@@ -313,6 +314,17 @@
     hess_ref[...] = hess[0, : KRY + 1]
 
 
+def reduce_groups(segs):
+    def number(place, inner):
+        seg, y = place
+        return seg * PEN + 16 * y + inner
+
+    places = [(seg, y) for seg in range(segs) for y in range(2)]
+    columns = [[number(place, inner) for inner in range(16)] for place in places]
+    planes = [[number(place, inner) for place in places] for inner in range(16)]
+    return columns, planes
+
+
 def body(state, krylov):
     pen = lax.axis_index("pen")
     segs = lax.axis_size("seg")
@@ -330,6 +342,10 @@
     exchange = functools.partial(
         lax.all_to_all, axis_name="pen", split_axis=0, concat_axis=0, tiled=True
     )
+    everywhere = functools.partial(
+        lax.all_to_all, axis_name=("seg", "pen"), split_axis=0, concat_axis=0, tiled=True
+    )
+    columns, planes = reduce_groups(segs)
     ring = [(s, (s + 1) % segs) for s in range(segs)]
 
     whole = pl.BlockSpec((CUT, PLANES, NX), lambda i: (0, 0, 0))
@@ -390,15 +406,17 @@
     base = lax.ppermute(ends[:, 0:36], "seg", ring)
     image, partial = call(
         dots_kernel,
-        [f32(CUT, PLANES, NX), f32(PEN, 8, TILE)],
+        [f32(CUT, PLANES, NX), f32(16, 8, TILE)],
         [tangent, kry_f, gram],
         [pltpu.VMEM((TILE, TILE), jnp.float32)],
         flops=1_000_000,
         moved=1_300_000,
     )
-    sums = jnp.sum(exchange(partial), axis=0)
-    sums = jnp.broadcast_to(sums[None], (segs, 8, TILE))
-    sums = lax.all_to_all(sums, "seg", 0, 0, tiled=True)
+    sums = everywhere(partial, axis_index_groups=columns)
+    sums = jnp.sum(sums, axis=0)
+    sums, base = lax.optimization_barrier((sums, base))
+    sums = jnp.broadcast_to(sums[None], (2 * segs, 8, TILE))
+    sums = everywhere(sums, axis_index_groups=planes)
     residual, vector, hess = call(
         finish_kernel,
         [f32(CUT, PLANES, NX)] * 2 + [f32(KRY + 1)],

time: 129 us -> 128 us (level)
  starting transfers between devices: 27.1 us -> 20.5 us
  blocking collectives: 66.7 us -> 70 us
  waiting for transfers between devices: 20.8 us -> 22.9 us
    all_to_all x1, waiting for transfers between devices: 0.01 us -> 5.65 us  [body(): sums = everywhere(partial, axis_index_groups=columns)]
    all_to_all x1, starting transfers between devices: 7.46 us -> 3.5 us  [body(): sums = everywhere(partial, axis_index_groups=columns)]
    ppermute x1, waiting for transfers between devices: 7.52 us -> 4.04 us  [body(): base = lax.ppermute(ends[:, 0:36], 'seg', ring)]
    all_to_all x1, blocking collectives: 13.3 us -> 16.7 us  [body(): sums = everywhere(sums, axis_index_groups=planes)]
    ppermute x1, starting transfers between devices: 4.72 us -> 2.11 us  [body(): base = lax.ppermute(ends[:, 0:36], 'seg', ring)]
  transfers between devices with their start and end apart: 4 -> 4, of which waited for: 3 -> 4; matrix products, arithmetic and copies ran while one was open for 0% -> 0% of each run, Pallas kernels for 2% -> 2%
where the time goes in v3:
time: 128 us; the launch traced here: 127 us
  blocking collectives  70 us (55%)
  waiting for transfers between devices  22.9 us (18%)
  starting transfers between devices  20.5 us (16%)
  Pallas kernels  12.4 us (10%)
    all_to_all x2, blocking collectives, body(): recv = exchange(send, axis_index_groups=TEAMS)  24.5 us
    all_to_all x2, blocking collectives, body(): recv = exchange(modes, axis_index_groups=TEAMS)  17 us
    all_to_all x1, blocking collectives, body(): sums = everywhere(sums, axis_index_groups=planes)  16.7 us
    all_to_all x1, blocking collectives, body(): ends = exchange(ends, axis_index_groups=PEERS)  11.9 us
    pallas_call x8, Pallas kernels, call(): pl.pallas_call(kernel, in_specs=[vmem] * len(operands), out_specs=[vmem]...  10.6 us
    all_to_all x1, starting transfers between devices, body(): packed = exchange(packed, axis_index_groups=PEERS)  10.4 us
    all_to_all x1, waiting for transfers between devices, body(): packed = exchange(packed, axis_index_groups=PEERS)  7.09 us
    ppermute x1, waiting for transfers between devices, body(): tangent = lax.ppermute(ends[:, 36:72], 'seg', ring)  6.15 us
  transfers between devices with their start and end apart: 4, of which 4 were waited for; matrix products, arithmetic and copies ran while one was open for 0% of the time, Pallas kernels for 2%

profile of v3, /device:TPU:8, one launch (start us, length us, event | category | flops | bytes accessed | tf_op | source)
XLA Modules:
  0.0 126.9 jit_solution(8199804081398457689)
XLA Ops:
  0.6 0.0 copy-start
  0.6 0.0 copy-start.7
  0.7 0.0 copy-start.6
  0.7 1.8 %shard_map.103 = f32[4,72,128]{2,1,0:T(8,128)} custom-call(f32[12,4,384]{2,1,0:T(4,128)} %bitcast.8, f32[16,12,4,384]{3,2,1,0:T(4,128)} %bitcast.4), custom_call_target="tpu_custom_call" | custom-call | tf_op jit(solution)/shard_map/pallas_call | solution.py:356
  2.4 0.0 copy-start.1
  2.4 0.0 copy-start.5
  2.4 10.4 %all-to-all-start = ((f32[4,72,128]{2,1,0:T(8,128)}), f32[4,72,128]{2,1,0:T(8,128)S(1)}, u32[]{:S(2)}, u32[]{:S(2)}) async-start(f32[4,72,128]{2,1,0:T(8,128)} %shard_map.103), calls=%async_computation | async-start | bytes 294912 | tf_op jit(solution)/shard_map/all_to_all | solution.py:365
  12.9 0.0 copy-done
  12.9 2.3 %shard_map.104.gram_ref = f32[8,128]{1,0:T(8,128)S(1)} custom-call(f32[16,12,4,384]{3,2,1,0:T(4,128)S(1)} %bitcast.5), custom_call_target="tpu_custom_call" | custom-call | flops 10000000 | bytes 1300000 | tf_op jit(solution)/shard_map/pallas_call | solution.py:102
  15.2 0.0 copy-done.7
  15.2 0.1 fusion.5
  15.3 0.0 copy-done.6
  15.3 0.1 fusion.3
  15.4 7.1 %all-to-all-done.recv_ref = f32[4,72,128]{2,1,0:T(8,128)S(1)} async-done(((f32[4,72,128]{2,1,0:T(8,128)}), f32[4,72,128]{2,1,0:T(8,128)S(1)}, u32[]{:S(2)}, u32[]{:S(2)}) %all-to-all-start) | async-done | bytes 147488 | tf_op jit(solution)/shard_map/all_to_all | solution.py:365
  22.5 0.0 copy-done.1
  22.5 0.0 copy-done.5
  22.5 1.0 shard_map.105
  23.4 0.0 copy-start.3
  23.4 0.0 copy-start.4
  23.5 12.2 %all_to_all.40.recv_ref = f32[8,144,128]{2,1,0:T(8,128)S(1)} all-to-all(f32[8,144,128]{2,1,0:T(8,128)S(1)} %get-tuple-element.17), channel_id=1, replica_groups={{0,1,2,3,16,17,18,19},{4,5,6,7,20,21,22,23},{8,9,10,11,24,25,26,27},{12..., dimensions={0} | all-to-all | bytes 1179648 | tf_op jit(solution)/shard_map/all_to_all | solution.py:380
  35.6 0.0 copy-done.3
  35.6 0.0 copy-done.4
  35.6 1.7 %shard_map.106 = f32[8,48,128]{2,1,0:T(8,128)S(1)} custom-call(f32[8,144,128]{2,1,0:T(8,128)S(1)} %all_to_all.40.recv_ref, bf16[768,384]{1,0:T(8,128)(2,1)S(1)} %copy-done.4, bf16[768,384]{1,0:T(8,128)(2,1)S(1)} %copy-done.3), custom_call_target="tpu_custom_call" | custom-call | flops 900000000 | bytes 2500000 | tf_op jit(solution)/shard_map/pallas_call | solution.py:102
  37.4 8.5 %all_to_all.41.recv_ref = f32[8,48,128]{2,1,0:T(8,128)S(1)} all-to-all(f32[8,48,128]{2,1,0:T(8,128)S(1)} %shard_map.106), channel_id=1, replica_groups={{0,1,2,3,16,17,18,19},{4,5,6,7,20,21,22,23},{8,9,10,11,24,25,26,27},{12..., dimensions={0} | all-to-all | bytes 393216 | tf_op jit(solution)/shard_map/all_to_all | solution.py:388
  45.9 1.3 %shard_map.107 = (f32[8,144,128]{2,1,0:T(8,128)S(1)}, f32[2,48,384]{2,1,0:T(8,128)S(1)}) custom-call(f32[8,48,128]{2,1,0:T(8,128)S(1)} %all_to_all.41.recv_ref, f32[2,48,384]{2,1,0:T(8,128)S(1)} %get-tuple-element.18.old_ref, f32[48,384]{1,0:T(8,128)S(1)} %get-tuple-element.31.damping_ref, f32[48,384]{1,0:T(8,128)S(1)} %get-tuple-element.32.inverse_ref, ...), custom_call_target="tpu_custom_call" | custom-call | flops 900000000 | bytes 3000000 | tf_op jit(solution)/shard_map/pallas_call | solution.py:102
  47.2 12.3 %all_to_all.42.recv_ref = f32[8,144,128]{2,1,0:T(8,128)S(1)} all-to-all(f32[8,144,128]{2,1,0:T(8,128)S(1)} %get-tuple-element.19), channel_id=1, replica_groups={{0,1,2,3,16,17,18,19},{4,5,6,7,20,21,22,23},{8,9,10,11,24,25,26,27},{12..., dimensions={0} | all-to-all | bytes 1179648 | tf_op jit(solution)/shard_map/all_to_all | solution.py:380
  59.5 1.7 %shard_map.108 = f32[8,48,128]{2,1,0:T(8,128)S(1)} custom-call(f32[8,144,128]{2,1,0:T(8,128)S(1)} %all_to_all.42.recv_ref, bf16[768,384]{1,0:T(8,128)(2,1)S(1)} %copy-done.4, bf16[768,384]{1,0:T(8,128)(2,1)S(1)} %copy-done.3), custom_call_target="tpu_custom_call" | custom-call | flops 900000000 | bytes 2500000 | tf_op jit(solution)/shard_map/pallas_call | solution.py:102
  61.2 8.5 %all_to_all.43.recv_ref = f32[8,48,128]{2,1,0:T(8,128)S(1)} all-to-all(f32[8,48,128]{2,1,0:T(8,128)S(1)} %shard_map.108), channel_id=1, replica_groups={{0,1,2,3,16,17,18,19},{4,5,6,7,20,21,22,23},{8,9,10,11,24,25,26,27},{12..., dimensions={0} | all-to-all | bytes 393216 | tf_op jit(solution)/shard_map/all_to_all | solution.py:388
  69.8 0.4 shard_map.109
  70.1 0.0 copy-start.2
  70.2 11.9 %all_to_all.44 = f32[4,72,128]{2,1,0:T(8,128)S(1)} all-to-all(f32[4,72,128]{2,1,0:T(8,128)S(1)} %shard_map.109), channel_id=1, replica_groups={{0,4,8,12},{1,5,9,13},{2,6,10,14},{3,7,11,15},{16,20,24,28},{17,21,25,2..., dimensions={0} | all-to-all | bytes 294912 | tf_op jit(solution)/shard_map/all_to_all | solution.py:404
  82.1 4.5 %collective-permute-start = (f32[4,36,128]{2,1,0:T(8,128)S(1)}, f32[4,36,128]{2,1,0:T(8,128)S(1)}, u32[]{:S(2)}, u32[]{:S(2)}) collective-permute-start(f32[4,36,128]{2,1,0:T(8,128)S(1)} %get-tuple-element.30), channel_id=1, source_target_pairs={{0,32},{32,64},{64,96},{96,128},{128,160},{160,192},{192,224},{224... | collective-permute-start | bytes 221192 | tf_op jit(solution)/shard_map/ppermute | solution.py:405
  86.6 6.2 %collective-permute-done.planes_ref = f32[4,36,128]{2,1,0:T(8,128)S(1)} collective-permute-done((f32[4,36,128]{2,1,0:T(8,128)S(1)}, f32[4,36,128]{2,1,0:T(8,128)S(1)}, u32[]{:S(2)}, u32[]{:S(2)}) %collective-permute-start) | collective-permute-done | bytes 73760 | tf_op jit(solution)/shard_map/ppermute | solution.py:405
  92.7 1.2 shard_map.110
  93.9 3.5 %all-to-all-start.6 = ((f32[16,8,128]{2,1,0:T(8,128)}), f32[16,8,128]{2,1,0:T(8,128)S(1)}, u32[]{:S(2)}, u32[]{:S(2)}) async-start(f32[16,8,128]{2,1,0:T(8,128)} %get-tuple-element.22), calls=%async_computation.6 | async-start | bytes 131072 | tf_op jit(solution)/shard_map/all_to_all | solution.py:415
  97.4 2.1 %collective-permute-start.1 = (f32[4,36,128]{2,1,0:T(8,128)S(1)}, f32[4,36,128]{2,1,0:T(8,128)S(1)}, u32[]{:S(2)}, u32[]{:S(2)}) collective-permute-start(f32[4,36,128]{2,1,0:T(8,128)S(1)} %get-tuple-element.29), channel_id=1, source_target_pairs={{0,32},{32,64},{64,96},{96,128},{128,160},{160,192},{192,224},{224... | collective-permute-start | bytes 221192 | tf_op jit(solution)/shard_map/ppermute | solution.py:406
  99.5 5.6 %all-to-all-done.6 = f32[16,8,128]{2,1,0:T(8,128)S(1)} async-done(((f32[16,8,128]{2,1,0:T(8,128)}), f32[16,8,128]{2,1,0:T(8,128)S(1)}, u32[]{:S(2)}, u32[]{:S(2)}) %all-to-all-start.6) | async-done | bytes 65568 | tf_op jit(solution)/shard_map/all_to_all | solution.py:415
  105.2 4.0 %collective-permute-done.1.planes_ref = f32[4,36,128]{2,1,0:T(8,128)S(1)} collective-permute-done((f32[4,36,128]{2,1,0:T(8,128)S(1)}, f32[4,36,128]{2,1,0:T(8,128)S(1)}, u32[]{:S(2)}, u32[]{:S(2)}) %collective-permute-start.1) | collective-permute-done | bytes 73760 | tf_op jit(solution)/shard_map/ppermute | solution.py:406
  109.2 16.7 %all_to_all.45.sums_ref = f32[32,8,128]{2,1,0:T(8,128)S(1)} all-to-all(f32[32,8,128]{2,1,0:T(8,128)S(1)} %broadcast_in_dim.5), channel_id=1, replica_groups={{0,16,32,48,64,80,96,112,128,144,160,176,192,208,224,240,256,272,288,30..., dimensions={0} | all-to-all | bytes 262144 | tf_op jit(solution)/shard_map/all_to_all | solution.py:419
  125.9 0.0 copy-done.2
  125.9 1.0 shard_map.111
  (3 shorter events, 0.0 us)
Async XLA Ops:
  0.6 12.2 %copy-start = (f32[16,4,12,384]{3,1,2,0:T(4,128)S(1)}, f32[16,4,12,384]{3,1,2,0:T(4,128)}, u32[]{:S(2)}) copy-start(f32[16,4,12,384]{3,1,2,0:T(4,128)} %param.9) | copy-start | bytes 3538948
  0.6 14.5 %copy-start.7 = (s32[48]{0:T(128)S(1)}, s32[48]{0:T(128)}, u32[]{:S(2)}) copy-start(s32[48]{0:T(128)} %constant.59.clone) | copy-start | bytes 580
  0.7 14.6 %copy-start.6 = (f32[384]{0:T(512)S(1)}, f32[384]{0:T(512)}, u32[]{:S(2)}) copy-start(f32[384]{0:T(512)} %constant.67) | copy-start | bytes 4612
  2.4 20.0 %copy-start.1 = (bf16[768,384]{1,0:T(8,128)(2,1)S(1)}, bf16[768,384]{1,0:T(8,128)(2,1)}, u32[]{:S(2)}) copy-start(bf16[768,384]{1,0:T(8,128)(2,1)} %constant.61.clone.cas_ref) | copy-start | bytes 1769476
  2.4 20.0 %copy-start.5 = (bf16[768,384]{1,0:T(8,128)(2,1)S(1)}, bf16[768,384]{1,0:T(8,128)(2,1)}, u32[]{:S(2)}) copy-start(bf16[768,384]{1,0:T(8,128)(2,1)} %constant.62.clone.slope_ref) | copy-start | bytes 1769476
  2.4 20.0 %all-to-all-start = ((f32[4,72,128]{2,1,0:T(8,128)}), f32[4,72,128]{2,1,0:T(8,128)S(1)}, u32[]{:S(2)}, u32[]{:S(2)}) async-start(f32[4,72,128]{2,1,0:T(8,128)} %shard_map.103), calls=%async_computation | async-start | bytes 294912 | tf_op jit(solution)/shard_map/all_to_all | solution.py:365
  23.4 12.2 %copy-start.3 = (bf16[768,384]{1,0:T(8,128)(2,1)S(1)}, bf16[768,384]{1,0:T(8,128)(2,1)}, u32[]{:S(2)}) copy-start(bf16[768,384]{1,0:T(8,128)(2,1)} %constant.64.clone.slope_ref) | copy-start | bytes 1769476
  23.4 12.2 %copy-start.4 = (bf16[768,384]{1,0:T(8,128)(2,1)S(1)}, bf16[768,384]{1,0:T(8,128)(2,1)}, u32[]{:S(2)}) copy-start(bf16[768,384]{1,0:T(8,128)(2,1)} %constant.63.clone.cas_ref) | copy-start | bytes 1769476
  70.1 55.8 %copy-start.2 = (f32[4,12,384]{2,0,1:T(4,128)S(1)}, f32[4,12,384]{2,0,1:T(4,128)}, u32[]{:S(2)}) copy-start(f32[4,12,384]{2,0,1:T(4,128)} %param.8) | copy-start | bytes 221188
  82.1 10.7 %collective-permute-start = (f32[4,36,128]{2,1,0:T(8,128)S(1)}, f32[4,36,128]{2,1,0:T(8,128)S(1)}, u32[]{:S(2)}, u32[]{:S(2)}) collective-permute-start(f32[4,36,128]{2,1,0:T(8,128)S(1)} %get-tuple-element.30), channel_id=1, source_target_pairs={{0,32},{32,64},{64,96},{96,128},{128,160},{160,192},{192,224},{224... | collective-permute-start | bytes 221192 | tf_op jit(solution)/shard_map/ppermute | solution.py:405
  93.9 11.3 %all-to-all-start.6 = ((f32[16,8,128]{2,1,0:T(8,128)}), f32[16,8,128]{2,1,0:T(8,128)S(1)}, u32[]{:S(2)}, u32[]{:S(2)}) async-start(f32[16,8,128]{2,1,0:T(8,128)} %get-tuple-element.22), calls=%async_computation.6 | async-start | bytes 131072 | tf_op jit(solution)/shard_map/all_to_all | solution.py:415
  97.4 11.8 %collective-permute-start.1 = (f32[4,36,128]{2,1,0:T(8,128)S(1)}, f32[4,36,128]{2,1,0:T(8,128)S(1)}, u32[]{:S(2)}, u32[]{:S(2)}) collective-permute-start(f32[4,36,128]{2,1,0:T(8,128)S(1)} %get-tuple-element.29), channel_id=1, source_target_pairs={{0,32},{32,64},{64,96},{96,128},{128,160},{160,192},{192,224},{224... | collective-permute-start | bytes 221192 | tf_op jit(solution)/shard_map/ppermute | solution.py:406
